TPU v7x, 32 devices: a whole 2x2x4 slice. The times are simulated.
32 devices in a mesh: segment: 4 (over z), expert: 2 (over y), dp: 4 (over x, core).
Axes of the slice: x: 2, y: 2, z: 4, core: 2. Of those that a mesh axis runs over, the one named last changes fastest.
Arguments:
- state_in: bfloat16 [4, 4, 1024, 2048], P('segment', None, ('expert', 'dp')), may hold values from -6 to 6
- entering: bfloat16 [1, 4, 1024, 2048], P(None, None, ('expert', 'dp')), may hold values from -6 to 6
- saved: bfloat16 [4, 2, 2, 1024, 2048], P('segment', None, None, ('expert', 'dp')), may hold values from -6 to 6
- route_ids: int32 [4, 2, 4, 2, 1024, 6], P('segment', None, None, None, ('expert', 'dp')), may hold values from 0 to 63, as said below
- gate_vals: float32 [4, 2, 4, 2, 1024, 6], P('segment', None, None, None, ('expert', 'dp')), may hold values from 0.25 to 1
- w_gate: bfloat16 [4, 2, 2048, 1408], P('segment', 'expert', None, 'dp'), may hold values from -0.125 to 0.125
- w_up: bfloat16 [4, 2, 2048, 1408], P('segment', 'expert', None, 'dp'), may hold values from -0.125 to 0.125
- w_down: bfloat16 [4, 2, 1408, 2048], P('segment', 'expert', 'dp'), may hold values from -0.15625 to 0.15625
- gains: float32 [4, 2, 2048], P('segment'), may hold values from 0.5 to 2
Outputs:
- state_out: bfloat16 [4, 4, 1024, 2048], P('segment', None, ('expert', 'dp'))
Inputs may be any that keep to these rules, and one draw needn't show every extreme that they name: `route_ids`: the ids of one token are distinct, and a token names at most one id under 1. Within each block of 128 consecutive tokens (the tokens of one device) an id under 1 is named by at most 8 tokens. For every section, slot, unit and sublayer some id under 1 is named by exactly 8 tokens in every block, and every block has an id under 1 named by exactly 8 of its tokens.
All inputs are finite; a program needn't handle non-finite values.
Results may differ from a plain program's by a relative error of at most 0.017.
Values may be sent and summed in bfloat16 or wider, within the bound.
A program may use at most 128 MiB of HBM per device.

v0:
```python
import functools
import jax
import jax.numpy as jnp
from jax import lax
from jax.experimental import pallas as pl
from jax.experimental.pallas import tpu as pltpu
from jax.sharding import PartitionSpec as P

CAP = 8
EPSILON = 1e-06
LAST = (((1,), (1,)), ((), ()))
MESH = pl.DeviceIdType.MESH
BF = jnp.bfloat16
F32 = jnp.float32
ITEMS_OUT = (3, 4, 2, 2, 1)
ITEMS_BACK = (3, 2, 2, 2, 1)


def mm(a, b):
    return jnp.dot(a, b, preferred_element_type=F32)


def mm_t(a, b):
    return lax.dot_general(a, b, LAST, preferred_element_type=F32)


def mix(overlap, rows):
    picks = overlap.astype(BF)
    high = rows.astype(BF)
    rest = rows - high.astype(F32)
    mid = rest.astype(BF)
    low = (rest - mid.astype(F32)).astype(BF)
    return mm(picks, high) + (mm(picks, mid) + mm(picks, low))


def unit_norm(rows, gain):
    inv = lax.rsqrt(jnp.mean(rows * rows, axis=-1, keepdims=True) + EPSILON)
    return (rows * inv * gain).astype(BF), inv


def back_norm(rows, inv, gain, grad):
    weighted = gain * grad
    total = jnp.sum(weighted * rows, axis=-1, keepdims=True)
    return inv * weighted - rows * (inv * inv * inv) * total / rows.shape[-1]


def kernel(sizes, state_in, entering, saved_in, ids, gates, wg_in, wu_in, wd_in, gains, out, *scratch):
    ns, ne, nd = sizes
    group = ne * nd
    ec = ne // 2
    width = ec * CAP
    tokens, model = state_in.shape[1], state_in.shape[2]
    outs, ins, back_outs, back_ins = scratch[0:5], scratch[5:10], scratch[10:15], scratch[15:20]
    (base, patch_out, patch_in, sel, gate_col, vals, pre, wg, wu, wd,
     send_sem, recv_sem, local_sem, relay_send, relay_recv, enter_sem, weight_sem, state, saved, input_sem) = scratch[20:]
    seg, ex, dp = lax.axis_index("segment"), lax.axis_index("expert"), lax.axis_index("dp")
    me = ex * nd + dp

    input_copies = [
        pltpu.make_async_copy(state_in, state, input_sem.at[0]),
        pltpu.make_async_copy(saved_in, saved, input_sem.at[1]),
    ]
    for copy in input_copies:
        copy.start()
    weight_copies = [
        pltpu.make_async_copy(source, dest, weight_sem.at[i])
        for i, (source, dest) in enumerate(((wg_in, wg), (wu_in, wu), (wd_in, wd)))
    ]
    for copy in weight_copies:
        copy.start()

    barrier = pltpu.get_barrier_semaphore()

    @pl.loop(1, group)
    def _(k):
        t = lax.rem(me + k, group)
        pl.semaphore_signal(
            barrier, inc=1, device_id=(seg, lax.div(t, nd), lax.rem(t, nd)), device_id_type=MESH
        )

    has_up, has_down = seg < ns - 1, seg > 0

    @pl.when(has_up)
    def _():
        pl.semaphore_signal(barrier, inc=1, device_id=(seg + 1, ex, dp), device_id_type=MESH)

    @pl.when(has_down)
    def _():
        pl.semaphore_signal(barrier, inc=1, device_id=(seg - 1, ex, dp), device_id_type=MESH)

    lane = lax.broadcasted_iota(jnp.int32, (tokens, tokens), 1)
    row = lax.broadcasted_iota(jnp.int32, (tokens, tokens), 0)
    before = (row < lane).astype(F32).astype(BF)
    eye = (row == lane).astype(F32)
    slot_row = lax.broadcasted_iota(jnp.int32, (CAP, tokens), 0).astype(F32)
    for e in range(ec):
        match = ids[...] == e
        routed = jnp.sum(match.astype(F32), axis=1)
        weight = jnp.sum(jnp.where(match, gates[...], 0.0), axis=1)
        earlier = mm(routed.astype(BF), before)
        for tb in range(ids.shape[0]):
            hit = (routed[tb:tb + 1] == 1.0) & (earlier[tb:tb + 1] == slot_row)
            one = jnp.where(hit, 1.0, 0.0)
            sel[tb, e * CAP:(e + 1) * CAP] = one
            gate_col[tb, e * CAP:(e + 1) * CAP] = jnp.broadcast_to(
                jnp.sum(one * weight[tb:tb + 1], axis=1, keepdims=True), (CAP, tokens)
            )

    neighbours = jnp.where(has_up, 1, 0) + jnp.where(has_down, 1, 0)
    pl.semaphore_wait(barrier, group - 1 + neighbours)

    def relay(unit, kind, source, dest):
        up = unit in (0, 3)
        goes, comes = (has_up, has_down) if up else (has_down, has_up)
        target = lax.rem(seg + (1 if up else ns - 1), ns)
        copy = pltpu.make_async_remote_copy(
            src_ref=source, dst_ref=dest, send_sem=relay_send.at[kind, unit],
            recv_sem=relay_recv.at[kind, unit], device_id=(target, ex, dp), device_id_type=MESH,
        )
        return goes, comes, copy

    def start_if(triple):
        @pl.when(triple[0])
        def _():
            triple[2].start()

    bulk = [relay(u, 0, state_in.at[u], base.at[u]) for u in range(4)]
    enter = [pltpu.make_async_copy(entering.at[u], base.at[u], enter_sem.at[u]) for u in range(4)]
    for u in range(4):
        start_if(bulk[u])

        @pl.when(jnp.logical_not(bulk[u][1]))
        def _(u=u):
            enter[u].start()

    def wait_bulk(u):
        @pl.when(bulk[u][1])
        def _():
            bulk[u][2].wait_recv()

        @pl.when(jnp.logical_not(bulk[u][1]))
        def _():
            enter[u].wait()

    patches = [relay(u, 1, patch_out.at[u], patch_in.at[u]) for u in range(4)]
    for u in range(4):
        @pl.when(jnp.logical_not(patches[u][1]))
        def _(u=u):
            patch_in[u] = jnp.zeros(patch_in.shape[1:], BF)

    def wait_patch(u):
        @pl.when(patches[u][1])
        def _():
            patches[u][2].wait_recv()

    def peer(t):
        return (seg, lax.div(t, nd), lax.rem(t, nd))

    def phase_of(r, outward, item):
        return sum(ITEMS_OUT[:r]) + item if outward else sum(ITEMS_OUT) + sum(ITEMS_BACK[:r]) + item

    def step_copy(r, k, outward, item, target):
        if outward:
            source, dest = outs[r].at[lax.div(target, nd), item], ins[r].at[me, item]
        else:
            source, dest = back_outs[r].at[target, item], back_ins[r].at[me, item]
        phase = phase_of(r, outward, item)
        return pltpu.make_async_remote_copy(
            src_ref=source, dst_ref=dest, send_sem=send_sem.at[phase, k],
            recv_sem=recv_sem.at[phase, k], device_id=peer(target), device_id_type=MESH,
        )

    def own_copy(r, outward, item):
        source = outs[r].at[ex, item] if outward else back_outs[r].at[me, item]
        dest = ins[r].at[me, item] if outward else back_ins[r].at[me, item]
        return pltpu.make_async_copy(source, dest, local_sem.at[phase_of(r, outward, item)])

    def send(r, outward, item):
        @pl.loop(1, group)
        def _(k):
            step_copy(r, k, outward, item, lax.rem(me + k, group)).start()

        own_copy(r, outward, item).start()

    def receive(r, outward, *items):
        arrived = ins[r] if outward else back_ins[r]
        for item in items:
            phase = phase_of(r, outward, item)

            @pl.loop(1, group)
            def _(k, item=item, phase=phase):
                slot = arrived.at[lax.rem(me - k + group, group), item]
                pltpu.make_async_remote_copy(
                    src_ref=slot, dst_ref=slot, send_sem=send_sem.at[phase, k],
                    recv_sem=recv_sem.at[phase, k], device_id=peer(me), device_id_type=MESH,
                ).wait_recv()

            own_copy(r, outward, item).wait()

    def drain(r, outward, item):
        @pl.loop(1, group)
        def _(k):
            step_copy(r, k, outward, item, lax.rem(me + k, group)).wait_send()

    def tab(slot, unit, sub):
        return (slot * 4 + unit) * 2 + sub

    def pick(slot, unit, values):
        first = unit % 2
        both = jnp.concatenate([sel[tab(slot, unit, first)], sel[tab(slot, unit, 1 - first)]])
        return mm(both.astype(BF), values)

    def pick_new(unit, old):
        first = unit % 2
        both = jnp.concatenate([sel[tab(1, unit, first)], sel[tab(1, unit, 1 - first)]])
        held = old[:, model:]
        keep = 1.0 - jnp.sum(held.astype(F32), axis=0, keepdims=True)
        moved = mm_t(both.astype(BF), held).astype(BF)
        return mm((both * keep).astype(BF), base[unit]) + mm(moved, old[:, :model])

    def overlap(slot, unit):
        first = unit % 2
        return mm_t(sel[tab(slot, unit, 1 - first)].astype(BF), sel[tab(slot, unit, first)].astype(BF))

    def overlap_t(slot, unit):
        first = unit % 2
        return mm_t(sel[tab(slot, unit, first)].astype(BF), sel[tab(slot, unit, 1 - first)].astype(BF))

    def gate(slot, unit, second):
        sub = 1 - unit % 2 if second else unit % 2
        return gate_col[tab(slot, unit, sub)][:, 0:1]

    def gain(unit, second):
        sub = 1 - unit % 2 if second else unit % 2
        return gains[sub:sub + 1]

    def put(r, item, unit, second, rows):
        side = 1 - unit % 2 if second else unit % 2
        for e in range(ec):
            outs[r][side * ec + e, item] = rows[e * CAP:(e + 1) * CAP].astype(BF)

    def got(r, item, unit, second):
        side = 1 - unit % 2 if second else unit % 2
        parts = []
        for e in range(ec):
            first = (side * ec + e) * nd
            total = back_ins[r][first, item].astype(F32)
            for q in range(1, nd):
                total = total + back_ins[r][first + q, item].astype(F32)
            parts.append(total)
        return parts[0] if ec == 1 else jnp.concatenate(parts)

    def rows_of(r, items):
        parts = [ins[r][:, i].astype(F32).reshape(group * CAP, model) for i in items]
        rows = parts[0] if len(parts) == 1 else jnp.concatenate(parts)
        return rows.astype(BF)

    def give(r, item, rows):
        back_outs[r][:, item] = rows.reshape(group, CAP, model).astype(BF)

    gr = group * CAP

    def half_forward(rows):
        return mm(rows, wg[...]), mm(rows, wu[...])

    def finish_forward(gp, up):
        return mm((gp * jax.nn.sigmoid(gp) * up).astype(BF), wd[...])

    def backward(rows, gp, up):
        act = mm_t(rows, wd[...])
        sig = jax.nn.sigmoid(gp)
        grad_gate = (act * up * sig * (1.0 + gp * (1.0 - sig))).astype(BF)
        grad_up = (act * gp * sig).astype(BF)
        return mm_t(grad_gate, wg[...]) + mm_t(grad_up, wu[...])

    names = ("fx1", "fx2", "k0a", "k0b", "k1a", "k1b", "d0a", "d0b", "d1a", "d1b", "g0", "g1")

    def at(name, st):
        return names.index(name) * 2 + st

    def forward_middle(slot, st, r, item):
        add = gate(slot, st, False) * got(r, item, st, False)
        vals[at("fx1", st)] = vals[at("fx1", st)] + add
        middle = vals[at("fx2", st)] + mix(overlap(slot, st), add)
        vals[at("fx2", st)] = middle
        return unit_norm(middle, gain(st, True))[0]

    def final_patch(slot, unit, first_rows, second_rows, last_second):
        a = unit % 2
        s1, s2 = sel[tab(slot, unit, a)], sel[tab(slot, unit, 1 - a)]
        if last_second:
            s1 = s1 * (1.0 - jnp.sum(s2, axis=0, keepdims=True))
        else:
            s2 = s2 * (1.0 - jnp.sum(s1, axis=0, keepdims=True))
        return (
            jnp.concatenate([first_rows, second_rows]).astype(BF),
            jnp.concatenate([s1, s2]).astype(BF),
        )

    def send_patch(unit, patch):
        patch_out[unit, :, :model] = patch[0]
        patch_out[unit, :, model:] = patch[1]
        start_if(patches[unit])

    def forward_end(slot, st, r, item):
        second = vals[at("fx2", st)] + gate(slot, st, True) * got(r, item, st, True)
        return final_patch(slot, st, vals[at("fx1", st)], second, True)

    def backward_middle(slot, st, r, item):
        b = 2 + st
        middle = vals[at(f"k{slot}b", st)]
        inv = unit_norm(middle, gain(b, True))[1]
        step = back_norm(middle, inv, gain(b, True), got(r, item, b, True))
        vals[at(f"d{slot}b", st)] = vals[at(f"d{slot}b", st)] + step
        inner = vals[at(f"d{slot}a", st)] + mix(overlap_t(slot, b), step)
        vals[at(f"d{slot}a", st)] = inner
        return gate(slot, b, False) * inner

    def backward_end(slot, st, r, item):
        b = 2 + st
        start = vals[at(f"k{slot}a", st)]
        inv = unit_norm(start, gain(b, False))[1]
        first = vals[at(f"d{slot}a", st)] + back_norm(start, inv, gain(b, False), got(r, item, b, False))
        return final_patch(slot, b, first, vals[at(f"d{slot}b", st)], False)

    def write(unit, patch):
        new_rows, new_sel = patch
        old = patch_in[unit]
        fresh = 1.0 - jnp.sum(new_sel.astype(F32), axis=0, keepdims=True)
        old_sel = old[:, model:].astype(F32) * fresh
        kept = eye * (fresh - jnp.sum(old_sel, axis=0, keepdims=True))
        spread = mm_t(eye.astype(BF), jnp.concatenate([old_sel.astype(BF), new_sel])).astype(BF)
        rows = jnp.concatenate([old[:, :model], new_rows])
        out[unit] = (mm(kept.astype(BF), base[unit]) + mm(spread, rows)).astype(BF)

    both_streams = range(2)

    def start_kept(slot, item):
        for st in both_streams:
            b = 2 + st
            both = pick(slot, b, saved[slot, st])
            vals[at(f"k{slot}a", st)], vals[at(f"k{slot}b", st)] = both[:width], both[width:]
            put(0, item, b, False, unit_norm(both[:width], gain(b, False))[0])
        send(0, True, item)

    def middle_kept(slot, item, to):
        receive(0, False, item)
        for st in both_streams:
            b = 2 + st
            add = gate(slot, b, False) * got(0, item, b, False)
            middle = vals[at(f"k{slot}b", st)] + mix(overlap(slot, b), add)
            vals[at(f"k{slot}b", st)] = middle
            put(1, to, b, True, unit_norm(middle, gain(b, True))[0])
        send(1, True, to)

    input_copies[0].wait()
    for st in both_streams:
        both = pick(0, st, state[st])
        vals[at("fx1", st)], vals[at("fx2", st)] = both[:width], both[width:]
        put(0, 0, st, False, unit_norm(both[:width], gain(st, False))[0])
    send(0, True, 0)
    input_copies[1].wait()
    start_kept(0, 1)
    for st in both_streams:
        both = pick(0, 2 + st, state[2 + st])
        vals[at("d0a", st)], vals[at("d0b", st)] = both[:width], both[width:]
        put(1, 2, 2 + st, True, gate(0, 2 + st, True) * both[width:])
    send(1, True, 2)
    for copy in weight_copies:
        copy.wait()
    receive(0, True, 0)
    gp, up = half_forward(rows_of(0, (0,)))
    give(0, 0, finish_forward(gp, up))
    send(0, False, 0)
    receive(0, True, 1)
    gp, up = half_forward(rows_of(0, (1,)))
    pre[0], pre[1] = gp, up
    give(0, 1, finish_forward(gp, up))
    send(0, False, 1)
    receive(0, False, 0)
    for st in both_streams:
        put(1, 0, st, True, forward_middle(0, st, 0, 0))
    send(1, True, 0)
    middle_kept(0, 1, 1)
    start_kept(1, 2)

    receive(1, True, 0)
    give(1, 0, finish_forward(*half_forward(rows_of(1, (0,)))))
    send(1, False, 0)
    receive(1, True, 1, 2)
    gp, up = half_forward(rows_of(1, (1,)))
    give(1, 1, backward(rows_of(1, (2,)), gp, up))
    send(1, False, 1)
    receive(0, True, 2)
    gp, up = half_forward(rows_of(0, (2,)))
    pre[2], pre[3] = gp, up
    give(0, 2, finish_forward(gp, up))
    send(0, False, 2)
    receive(1, False, 0)
    for st in both_streams:
        send_patch(st, forward_end(0, st, 1, 0))
    receive(1, False, 1)
    for st in both_streams:
        put(2, 0, 2 + st, False, backward_middle(0, st, 1, 1))
    send(2, True, 0)

    for st in both_streams:
        wait_bulk(st)
        wait_patch(st)
        both = pick_new(st, patch_in[st])
        vals[at("fx1", st)], vals[at("fx2", st)] = both[:width], both[width:]
        put(2, 1, st, False, unit_norm(both[:width], gain(st, False))[0])
    send(2, True, 1)
    middle_kept(1, 2, 3)
    receive(2, True, 0)
    give(2, 0, backward(rows_of(2, (0,)), pre[0], pre[1]))
    send(2, False, 0)
    receive(2, True, 1)
    give(2, 1, finish_forward(*half_forward(rows_of(2, (1,)))))
    send(2, False, 1)
    receive(1, True, 3)
    pre[4], pre[5] = half_forward(rows_of(1, (3,)))
    receive(2, False, 0)
    for st in both_streams:
        send_patch(2 + st, backward_end(0, st, 2, 0))
    receive(2, False, 1)
    for st in both_streams:
        put(3, 0, st, True, forward_middle(1, st, 2, 1))

    for st in both_streams:
        u = 2 + st
        wait_bulk(u)
        wait_patch(u)
        both = pick_new(u, patch_in[u])
        vals[at("d1a", st)], vals[at("d1b", st)] = both[:width], both[width:]
        put(3, 1, u, True, gate(1, u, True) * both[width:])
    send(3, True, 1)
    send(3, True, 0)
    receive(3, True, 1)
    give(3, 1, backward(rows_of(3, (1,)), pre[4], pre[5]))
    send(3, False, 1)
    receive(3, True, 0)
    give(3, 0, finish_forward(*half_forward(rows_of(3, (0,)))))
    send(3, False, 0)
    receive(3, False, 1)
    for st in both_streams:
        put(4, 0, 2 + st, False, backward_middle(1, st, 3, 1))
    send(4, True, 0)
    receive(3, False, 0)
    for st in both_streams:
        write(st, forward_end(1, st, 3, 0))
    receive(4, True, 0)
    give(4, 0, backward(rows_of(4, (0,)), pre[2], pre[3]))
    send(4, False, 0)
    receive(4, False, 0)
    for st in both_streams:
        write(2 + st, backward_end(1, st, 4, 0))

    for r in range(5):
        for item in range(ITEMS_OUT[r]):
            drain(r, True, item)
        for item in range(ITEMS_BACK[r]):
            drain(r, False, item)
    for triple in bulk + patches:
        @pl.when(triple[0])
        def _(triple=triple):
            triple[2].wait_send()


def local(sizes, state_in, entering, saved, route_ids, gate_vals, w_gate, w_up, w_down, gains):
    ns, ne, nd = sizes
    group, width = ne * nd, ne // 2 * CAP
    units, tokens, model = state_in.shape[1:]
    hidden = w_gate.shape[-1]
    tables = route_ids.shape[1] * route_ids.shape[2] * route_ids.shape[3]
    topk = route_ids.shape[-1]
    ids = jnp.swapaxes(route_ids.reshape(tables, tokens, topk), 1, 2)
    gates = jnp.swapaxes(gate_vals.reshape(tables, tokens, topk), 1, 2)
    vmem = pl.BlockSpec(memory_space=pltpu.VMEM)
    anywhere = pl.BlockSpec(memory_space=pl.ANY)
    dma = pltpu.SemaphoreType.DMA
    scratch = (
        [pltpu.VMEM((ne, n, CAP, model), BF) for n in ITEMS_OUT]
        + [pltpu.VMEM((group, n, CAP, model), BF) for n in ITEMS_OUT]
        + [pltpu.VMEM((group, n, CAP, model), BF) for n in ITEMS_BACK]
        + [pltpu.VMEM((group, n, CAP, model), BF) for n in ITEMS_BACK]
        + [
            pltpu.VMEM((units, tokens, model), BF),
            pltpu.VMEM((units, 2 * width, model + tokens), BF),
            pltpu.VMEM((units, 2 * width, model + tokens), BF),
            pltpu.VMEM((tables, width, tokens), F32),
            pltpu.VMEM((tables, width, tokens), F32),
            pltpu.VMEM((24, width, model), F32),
            pltpu.VMEM((6, group * CAP, hidden), F32),
            pltpu.VMEM((model, hidden), BF),
            pltpu.VMEM((model, hidden), BF),
            pltpu.VMEM((hidden, model), BF),
            dma((22, group)), dma((22, group)), dma((22,)),
            dma((2, units)), dma((2, units)), dma((units,)), dma((3,)),
            pltpu.VMEM((units, tokens, model), BF),
            pltpu.VMEM(saved.shape[1:], BF),
            dma((2,)),
        ]
    )
    result = pl.pallas_call(
        functools.partial(kernel, sizes),
        out_shape=jax.ShapeDtypeStruct((units, tokens, model), BF),
        in_specs=[anywhere, anywhere, anywhere, vmem, vmem, anywhere, anywhere, anywhere, vmem],
        out_specs=vmem,
        scratch_shapes=scratch,
        compiler_params=pltpu.CompilerParams(
            collective_id=0, has_side_effects=True, vmem_limit_bytes=67043328
        ),
    )(state_in[0], entering[0], saved[0], ids, gates, w_gate[0, 0], w_up[0, 0], w_down[0, 0], gains[0])
    return result[None]


def solution(mesh):
    in_specs = (
        P("segment", None, ("expert", "dp"), None),
        P(None, None, ("expert", "dp"), None),
        P("segment", None, None, ("expert", "dp"), None),
        P("segment", None, None, None, ("expert", "dp"), None),
        P("segment", None, None, None, ("expert", "dp"), None),
        P("segment", "expert", None, "dp"),
        P("segment", "expert", None, "dp"),
        P("segment", "expert", "dp", None),
        P("segment", None, None),
    )
    out_specs = P("segment", None, ("expert", "dp"), None)
    sizes = (mesh.shape["segment"], mesh.shape["expert"], mesh.shape["dp"])
    body = functools.partial(local, sizes)
    return jax.shard_map(body, mesh=mesh, in_specs=in_specs, out_specs=out_specs, check_vma=False)
```

profile of v0, /device:TPU:0, one launch (start us, length us, event | category | flops | bytes accessed | tf_op | source)
XLA Modules:
  0.0 96.6 jit_solution(12688548829945891079)
XLA Ops:
  0.0 0.0 copy-start
  0.0 1.5 %copy.10 = s32[1,2,4,2,128,6]{4,5,3,2,1,0:T(8,128)} copy(s32[1,2,4,2,128,6]{4,3,5,2,1,0:T(2,128)} %param.12) | data formatting | bytes 98304 | tf_op args[3]
  1.5 1.4 %copy.11 = f32[1,2,4,2,128,6]{4,5,3,2,1,0:T(8,128)} copy(f32[1,2,4,2,128,6]{4,3,5,2,1,0:T(2,128)} %param.13) | data formatting | bytes 98304 | tf_op args[4]
  3.0 2.6 %copy.12 = bf16[1,1,2048,352]{3,2,1,0:T(8,128)(2,1)} copy(bf16[1,1,2048,352]{2,3,1,0:T(8,128)(2,1)} %param.14) | data formatting | bytes 2883584 | tf_op args[5]
  5.5 0.0 copy-done
  5.5 1.6 %copy.13 = bf16[1,1,2048,352]{3,2,1,0:T(8,128)(2,1)} copy(bf16[1,1,2048,352]{2,3,1,0:T(8,128)(2,1)S(1)} %copy-done) | data formatting | bytes 2883584 | tf_op args[6]
  7.1 86.3 %shard_map.91 = bf16[4,128,2048]{2,1,0:T(8,128)(2,1)} custom-call(bf16[4,128,2048]{2,1,0:T(8,128)(2,1)} %bitcast.17, bf16[4,128,2048]{2,1,0:T(8,128)(2,1)} %bitcast.18, bf16[2,2,128,2048]{3,2,1,0:T(8,128)(2,1)} %bitcast.19, s32[16,6,128]{2,1,0:T(8,128)} %bitcast.21, f32[16,6,128]{2,1,0:T(8,128)} %bitcast.22, bf16[2048,352]{1,0:T(8,128)(2,1)} %bitcast.15, ...), custom_call_target="tpu_custom_call" | custom-call | tf_op jit(solution)/shard_map/pallas_call | solution.py:505
  93.4 3.2 %copy.15 = bf16[1,4,128,2048]{3,2,1,0:T(8,128)(2,1)} copy(bf16[1,4,128,2048]{3,2,1,0:T(8,128)(2,1)} %bitcast.14) | data formatting | bytes 4194304
Async XLA Ops:
  0.0 5.5 %copy-start = (bf16[1,1,2048,352]{2,3,1,0:T(8,128)(2,1)S(1)}, bf16[1,1,2048,352]{2,3,1,0:T(8,128)(2,1)}, u32[]{:S(2)}) copy-start(bf16[1,1,2048,352]{2,3,1,0:T(8,128)(2,1)} %param.15) | copy-start | bytes 4325380
where the time goes:
time: 96.8 us; the launch traced here: 96.6 us
  Pallas kernels  86.3 us (89%)
  local copies, waits for them, and re-layouts  10.2 us (11%)
    pallas_call x1, Pallas kernels, local(): pl.pallas_call(functools.partial(kernel, sizes), out_shape=jax.ShapeDtype...  86.3 us
    unnamed x7, local copies, waits for them, and re-layouts  10.2 us

commit v1 on v0

v1 whole, which is shorter than its diff:
```python
import functools
import jax
import jax.numpy as jnp
from jax import lax
from jax.experimental import pallas as pl
from jax.experimental.pallas import tpu as pltpu
from jax.sharding import PartitionSpec as P

CAP = 8
EPSILON = 1e-06
LAST = (((1,), (1,)), ((), ()))
MESH = pl.DeviceIdType.MESH
BF = jnp.bfloat16
F32 = jnp.float32
OUT = ("k0a", "f00", "d0b", "k1a", "k0b", "f01", "k1b", "d0a", "f10", "d1b", "f11", "d1a")
BACK = ("k0a", "f00", "k1a", "d0b", "f01", "d0a", "f10", "d1b", "f11", "d1a")
VALS = ("fx1", "fx2", "k0a", "k0b", "k1a", "k1b", "d0a", "d0b", "d1a", "d1b")
INVS = ("0a", "0b", "1a", "1b")
PRES = ("k0a", "k0b", "k1a", "k1b")
STREAMS = range(2)


def mm(a, b):
    return jnp.dot(a, b, preferred_element_type=F32)


def mm_t(a, b):
    return lax.dot_general(a, b, LAST, preferred_element_type=F32)


def mix(picks, rows):
    high = rows.astype(BF).astype(F32)
    rest = rows - high
    mid = rest.astype(BF).astype(F32)
    parts = jnp.concatenate([high, mid, rest - mid])
    return mm(picks.astype(BF), parts.astype(BF))


def unit_norm(rows, gain):
    inv = lax.rsqrt(jnp.mean(rows * rows, axis=-1, keepdims=True) + EPSILON)
    return rows * inv * gain, inv


def back_norm(rows, inv, gain, grad):
    weighted = gain * grad
    total = jnp.sum(weighted * rows, axis=-1, keepdims=True)
    return inv * weighted - rows * (inv * inv * inv) * total / rows.shape[-1]


def quotient(a, b):
    return a // b if isinstance(a, int) else lax.div(a, b)


def remainder(a, b):
    return a % b if isinstance(a, int) else lax.rem(a, b)


def kernel(sizes, state_in, entering, saved_in, ids, gates, wg_in, wu_in, wd_in, gains,
           pre_out, rows_out, spread_out,
           outs, ins, bouts, bins, base, final, state, saved, patch_out, patch_in, held_out, held_in,
           sel, gate_col, overlaps, moves, fresh_base, vals, invs, pre, early, wg, wu, wd,
           send_sem, recv_sem, local_sem, relay_send, relay_recv, enter_sem, weight_sem,
           pair_send, pair_recv, input_sem, pre_sem):
    ns, ne, nd = sizes
    nh = nd // 2
    group = ne * nh
    ec = ne // 2
    width = ec * CAP
    tokens, model = state_in.shape[1], state_in.shape[2]
    hidden = wg_in.shape[0]
    seg, ex, dp = lax.axis_index("segment"), lax.axis_index("expert"), lax.axis_index("dp")
    half, side = lax.div(dp, 2), lax.rem(dp, 2)
    me = ex * nh + half

    saved_copies = [pltpu.make_async_copy(saved_in.at[s], saved.at[s], input_sem.at[s]) for s in range(2)]
    state_copies = [
        pltpu.make_async_copy(state_in.at[pl.ds(2 * i, 2)], state.at[pl.ds(2 * i, 2)], input_sem.at[2 + i])
        for i in range(2)
    ]
    for copy in (saved_copies[0], state_copies[0], state_copies[1]):
        copy.start()

    barrier = pltpu.get_barrier_semaphore()

    def each_peer(body):
        if group <= 8:
            for k in reversed(range(1, group)):
                body(k)
        else:
            pl.loop(1, group)(body)

    def peer(k):
        te = lax.rem(ex + quotient(k, nh), ne)
        th = lax.rem(half + remainder(k, nh), nh)
        return te, th, (seg, te, th * 2 + side)

    def source_of(k):
        te = lax.rem(ex - quotient(k, nh) + ne, ne)
        th = lax.rem(half - remainder(k, nh) + nh, nh)
        return te * nh + th

    partner = (seg, ex, half * 2 + 1 - side)
    has_up, has_down = seg < ns - 1, seg > 0

    def greet(k):
        pl.semaphore_signal(barrier, inc=1, device_id=peer(k)[2], device_id_type=MESH)

    each_peer(greet)
    pl.semaphore_signal(barrier, inc=1, device_id=partner, device_id_type=MESH)

    @pl.when(has_up)
    def _():
        pl.semaphore_signal(barrier, inc=1, device_id=(seg + 1, ex, dp), device_id_type=MESH)

    @pl.when(has_down)
    def _():
        pl.semaphore_signal(barrier, inc=1, device_id=(seg - 1, ex, dp), device_id_type=MESH)

    weights = ((wg_in, wg), (wu_in, wu), (wd_in, wd))
    weight_copies = [
        pltpu.make_async_copy(source, dest.at[pl.ds(0, hidden)], weight_sem.at[i])
        for i, (source, dest) in enumerate(weights)
    ]
    pair_copies = [
        pltpu.make_async_remote_copy(
            src_ref=source, dst_ref=dest.at[pl.ds(hidden, hidden)], send_sem=pair_send.at[i],
            recv_sem=pair_recv.at[i], device_id=partner, device_id_type=MESH,
        )
        for i, (source, dest) in enumerate(weights)
    ]
    for copy in weight_copies:
        copy.start()
    saved_copies[1].start()

    units = state_in.shape[0]
    lane = lax.broadcasted_iota(jnp.int32, (tokens, tokens), 1)
    row = lax.broadcasted_iota(jnp.int32, (tokens, tokens), 0)
    before = (row < lane).astype(F32).astype(BF)
    eye = (row == lane).astype(F32)
    slot_row = lax.broadcasted_iota(jnp.int32, (CAP, tokens), 0).astype(F32)
    su = 2 * units
    topk = ids.shape[0] // (2 * su)

    def tab(slot, unit, sub):
        return sub * su + slot * units + unit

    for e in range(ec):
        routed, weight = [], []
        for j in range(2):
            count, total = jnp.zeros((su, tokens), F32), jnp.zeros((su, tokens), F32)
            for k in range(topk):
                rows = pl.ds(k * 2 + j, su, stride=2 * topk)
                match = ids[rows, :] == e
                count = count + match.astype(F32)
                total = total + jnp.where(match, gates[rows, :], 0.0)
            routed.append(count)
            weight.append(total)
        routed = jnp.concatenate(routed)
        weight = jnp.concatenate(weight)
        earlier = mm(routed.astype(BF), before)
        for tb in range(2 * su):
            hit = (routed[tb:tb + 1] == 1.0) & (earlier[tb:tb + 1] == slot_row)
            one = jnp.where(hit, 1.0, 0.0)
            sel[tb, e * CAP:(e + 1) * CAP] = one
            gate_col[tb, e * CAP:(e + 1) * CAP] = jnp.broadcast_to(
                jnp.sum(one * weight[tb:tb + 1], axis=1, keepdims=True), (CAP, tokens)
            )

    neighbours = jnp.where(has_up, 1, 0) + jnp.where(has_down, 1, 0)
    pl.semaphore_wait(barrier, group + neighbours)
    for copy in pair_copies:
        copy.start()

    def first_second(slot, unit):
        first = unit % 2
        return sel[tab(slot, unit, first)], sel[tab(slot, unit, 1 - first)]

    def last_picks(slot, unit):
        s1, s2 = first_second(slot, unit)
        if unit < 2:
            s1 = s1 * (1.0 - jnp.sum(s2, axis=0, keepdims=True))
        else:
            s2 = s2 * (1.0 - jnp.sum(s1, axis=0, keepdims=True))
        return jnp.concatenate([s1, s2])

    def both_picks(slot, unit):
        return jnp.concatenate(first_second(slot, unit))

    def pick(slot, unit, values):
        return mm(both_picks(slot, unit).astype(BF), values)

    def gate(slot, unit, second):
        sub = 1 - unit % 2 if second else unit % 2
        return gate_col[tab(slot, unit, sub)][:, 0:1]

    def gain(unit, second):
        sub = 1 - unit % 2 if second else unit % 2
        return gains[sub:sub + 1]

    def relay(unit, kind, source, dest):
        up = unit in (0, 3)
        goes, comes = (has_up, has_down) if up else (has_down, has_up)
        target = lax.rem(seg + (1 if up else ns - 1), ns)
        copy = pltpu.make_async_remote_copy(
            src_ref=source, dst_ref=dest, send_sem=relay_send.at[kind, unit],
            recv_sem=relay_recv.at[kind, unit], device_id=(target, ex, dp), device_id_type=MESH,
        )
        return goes, comes, copy

    def start_if(triple):
        @pl.when(triple[0])
        def _():
            triple[2].start()

    def arrive_if(triple):
        @pl.when(triple[1])
        def _():
            triple[2].wait_recv()

    bulk = [relay(u, 0, state_in.at[u], base.at[u]) for u in range(4)]
    enter = [pltpu.make_async_copy(entering.at[u], base.at[u], enter_sem.at[u]) for u in range(4)]
    patches = [relay(u, 1, patch_out.at[u], patch_in.at[u]) for u in range(4)]
    helds = [relay(u, 2, held_out.at[u], held_in.at[u]) for u in range(4)]

    def wait_bulk(u):
        arrive_if(bulk[u])

        @pl.when(jnp.logical_not(bulk[u][1]))
        def _():
            enter[u].wait()

    def out_copy(name, k):
        i = OUT.index(name)
        te, th, device = peer(k)
        return pltpu.make_async_remote_copy(
            src_ref=outs.at[i, te], dst_ref=ins.at[i, me], send_sem=send_sem.at[i, k],
            recv_sem=recv_sem.at[i, k], device_id=device, device_id_type=MESH,
        )

    def back_copy(name, k):
        i = BACK.index(name)
        te, th, device = peer(k)
        return pltpu.make_async_remote_copy(
            src_ref=bouts.at[i, te * nh + th], dst_ref=bins.at[i, me], send_sem=send_sem.at[len(OUT) + i, k],
            recv_sem=recv_sem.at[len(OUT) + i, k], device_id=device, device_id_type=MESH,
        )

    def own_out(name):
        i = OUT.index(name)
        return pltpu.make_async_copy(outs.at[i, ex], ins.at[i, me], local_sem.at[i])

    def own_back(name):
        i = BACK.index(name)
        return pltpu.make_async_copy(bouts.at[i, me], bins.at[i, me], local_sem.at[len(OUT) + i])

    def send_out(name):
        each_peer(lambda k: out_copy(name, k).start())
        own_out(name).start()

    def send_back(name):
        each_peer(lambda k: back_copy(name, k).start())
        own_back(name).start()

    def arrived(buffer, i, phase):
        def body(k):
            slot = buffer.at[i, source_of(k)]
            pltpu.make_async_remote_copy(
                src_ref=slot, dst_ref=slot, send_sem=send_sem.at[phase, k],
                recv_sem=recv_sem.at[phase, k], device_id=peer(k)[2], device_id_type=MESH,
            ).wait_recv()

        each_peer(body)

    def take_out(name):
        i = OUT.index(name)
        own_out(name).wait()
        arrived(ins, i, i)

    def take_back(name):
        i = BACK.index(name)
        own_back(name).wait()
        arrived(bins, i, len(OUT) + i)

    def put(name, unit, second, rows):
        j = 1 - unit % 2 if second else unit % 2
        for e in range(ec):
            outs[OUT.index(name), j * ec + e] = rows[e * CAP:(e + 1) * CAP].astype(BF)

    def got(name, unit, second):
        j = 1 - unit % 2 if second else unit % 2
        i = BACK.index(name)
        parts = []
        for e in range(ec):
            first = (j * ec + e) * nh
            total = bins[i, first].astype(F32)
            for q in range(1, nh):
                total = total + bins[i, first + q].astype(F32)
            parts.append(total)
        return parts[0] if ec == 1 else jnp.concatenate(parts)

    def rows_of(name):
        return ins[OUT.index(name)].astype(F32).reshape(group * CAP, model).astype(BF)

    def give(name, rows):
        bouts[BACK.index(name)] = rows.reshape(group, CAP, model).astype(BF)

    def half_forward(rows):
        return mm_t(rows, wg[...]), mm_t(rows, wu[...])

    def finish_forward(gp, up):
        return mm((gp * jax.nn.sigmoid(gp) * up).astype(BF), wd[...])

    def backward(act, gp, up):
        sig = jax.nn.sigmoid(gp)
        grad_gate = (act * up * sig * (1.0 + gp * (1.0 - sig))).astype(BF)
        grad_up = (act * gp * sig).astype(BF)
        return mm(grad_gate, wg[...]) + mm(grad_up, wu[...])

    def at(name, st):
        return VALS.index(name) * 2 + st

    def inv_at(slot, which, st):
        return INVS.index(f"{slot}{which}") * 2 + st

    def keep_inv(slot, which, st, inv):
        invs[inv_at(slot, which, st)] = jnp.broadcast_to(inv, (width, tokens))

    def held_inv(slot, which, st):
        return invs[inv_at(slot, which, st)][:, 0:1]

    def pre_at(name):
        i = PRES.index(name) * 2
        return pre[i], pre[i + 1]

    def keep_pre(name, values):
        i = PRES.index(name) * 2
        pre[i], pre[i + 1] = values

    def crossing(slot, unit, transposed):
        s1, s2 = first_second(slot, unit)
        if transposed:
            s1, s2 = s2, s1
        return mm_t(s2.astype(BF), jnp.concatenate([s1, s1, s1]).astype(BF))

    def over_at(slot, unit, transposed):
        return slot * 6 + unit + (2 if transposed else 0)

    def start_kept(slot):
        name = f"k{slot}a"
        saved_copies[slot].wait()
        for st in STREAMS:
            b = 2 + st
            both = pick(slot, b, saved[slot, st])
            vals[at(f"k{slot}a", st)], vals[at(f"k{slot}b", st)] = both[:width], both[width:]
            rows, inv = unit_norm(both[:width], gain(b, False))
            put(name, b, False, rows)
            keep_inv(slot, "a", st, inv)
        send_out(name)

    def middle_kept(slot):
        take_back(f"k{slot}a")
        for st in STREAMS:
            b = 2 + st
            add = gate(slot, b, False) * got(f"k{slot}a", b, False)
            middle = vals[at(f"k{slot}b", st)] + mix(overlaps[over_at(slot, b, False)], add)
            vals[at(f"k{slot}b", st)] = middle
            rows, inv = unit_norm(middle, gain(b, True))
            put(f"k{slot}b", b, True, rows)
            keep_inv(slot, "b", st, inv)
        send_out(f"k{slot}b")

    def forward_start(slot, st, first, second):
        vals[at("fx1", st)], vals[at("fx2", st)] = first, second
        put(f"f{slot}0", st, False, unit_norm(first, gain(st, False))[0])

    def forward_middle(slot):
        take_back(f"f{slot}0")
        for st in STREAMS:
            add = gate(slot, st, False) * got(f"f{slot}0", st, False)
            vals[at("fx1", st)] = vals[at("fx1", st)] + add
            middle = vals[at("fx2", st)] + mix(overlaps[over_at(slot, st, False)], add)
            vals[at("fx2", st)] = middle
            put(f"f{slot}1", st, True, unit_norm(middle, gain(st, True))[0])
        send_out(f"f{slot}1")

    def forward_end(slot, st, dest):
        second = vals[at("fx2", st)] + gate(slot, st, True) * got(f"f{slot}1", st, True)
        dest[st] = jnp.concatenate([vals[at("fx1", st)], second]).astype(BF)

    def backward_start(slot, st, first, second):
        vals[at(f"d{slot}a", st)], vals[at(f"d{slot}b", st)] = first, second
        put(f"d{slot}b", 2 + st, True, gate(slot, 2 + st, True) * second)

    def backward_middle(slot):
        take_back(f"d{slot}b")
        for st in STREAMS:
            b = 2 + st
            step = back_norm(
                vals[at(f"k{slot}b", st)], held_inv(slot, "b", st), gain(b, True), got(f"d{slot}b", b, True)
            )
            inner = vals[at(f"d{slot}a", st)] + mix(overlaps[over_at(slot, b, True)], step)
            put(f"d{slot}a", b, False, gate(slot, b, False) * inner)
            vals[at(f"d{slot}b", st)] = vals[at(f"d{slot}b", st)] + step
            vals[at(f"d{slot}a", st)] = inner
        send_out(f"d{slot}a")

    def backward_end(slot, st, dest):
        b = 2 + st
        first = vals[at(f"d{slot}a", st)] + back_norm(
            vals[at(f"k{slot}a", st)], held_inv(slot, "a", st), gain(b, False), got(f"d{slot}a", b, False)
        )
        dest[b] = jnp.concatenate([first, vals[at(f"d{slot}b", st)]]).astype(BF)

    def expert_forward(name, kept=False):
        take_out(name)
        gp, up = half_forward(rows_of(name))
        if kept:
            keep_pre(name, (gp, up))
        give(name, finish_forward(gp, up))
        send_back(name)

    def expert_backward(name, pres):
        take_out(name)
        give(name, backward(mm_t(rows_of(name), wd[...]), *pre_at(pres)))
        send_back(name)

    def ready_unit(u):
        wait_bulk(u)
        arrive_if(helds[u])
        held = held_in[u].astype(F32)
        both = both_picks(1, u)
        keep = 1.0 - jnp.sum(held, axis=0, keepdims=True)
        moves[u] = mm_t(both.astype(BF), held.astype(BF))
        fresh_base[u] = mm((both * keep).astype(BF), base[u])

    def pick_new(u):
        arrive_if(patches[u])
        return fresh_base[u] + mm(moves[u].astype(BF), patch_in[u])

    pre_copies = [pltpu.make_async_copy(final.at[u], pre_out.at[u], pre_sem.at[u]) for u in range(4)]

    def settle(u):
        new_sel = last_picks(1, u)
        fresh = 1.0 - jnp.sum(new_sel, axis=0, keepdims=True)
        old_sel = held_in[u].astype(F32) * fresh
        kept = eye * (fresh - jnp.sum(old_sel, axis=0, keepdims=True))
        spread = mm_t(eye.astype(BF), jnp.concatenate([old_sel, new_sel]).astype(BF))
        spread_out[u] = spread[:, 2 * width:].astype(BF)
        final[u] = (mm(kept.astype(BF), base[u]) + mm(spread[:, :2 * width].astype(BF), patch_in[u])).astype(BF)
        pre_copies[u].start()

    start_kept(0)
    state_copies[0].wait()
    for st in STREAMS:
        both = pick(0, st, state[st])
        forward_start(0, st, both[:width], both[width:])
    send_out("f00")
    state_copies[1].wait()
    for st in STREAMS:
        both = pick(0, 2 + st, state[2 + st])
        backward_start(0, st, both[:width], both[width:])
    send_out("d0b")

    for u in range(4):
        held_out[u] = last_picks(0, u).astype(BF)
    for u in range(4):
        start_if(helds[u])

        @pl.when(jnp.logical_not(helds[u][1]))
        def _(u=u):
            patch_in[u] = jnp.zeros(patch_in.shape[1:], BF)
            held_in[u] = jnp.zeros(held_in.shape[1:], BF)
    for u in range(4):
        start_if(bulk[u])

        @pl.when(jnp.logical_not(bulk[u][1]))
        def _(u=u):
            enter[u].start()
    for slot in range(2):
        for u in range(4):
            overlaps[over_at(slot, u, False)] = crossing(slot, u, False)
            if u >= 2:
                overlaps[over_at(slot, u, True)] = crossing(slot, u, True)

    for i in range(3):
        weight_copies[i].wait()
        pair_copies[i].wait_recv()
    expert_forward("k0a", True)
    expert_forward("f00")
    start_kept(1)
    take_out("d0b")
    early[...] = mm_t(rows_of("d0b"), wd[...])
    middle_kept(0)
    forward_middle(0)
    expert_forward("k1a", True)
    take_out("k0b")
    give("d0b", backward(early[...], *half_forward(rows_of("k0b"))))
    send_back("d0b")
    expert_forward("f01")
    middle_kept(1)
    backward_middle(0)
    take_back("f01")
    for st in STREAMS:
        forward_end(0, st, patch_out)
    for st in STREAMS:
        start_if(patches[st])
    take_out("k1b")
    keep_pre("k1b", half_forward(rows_of("k1b")))
    expert_backward("d0a", "k0a")
    for st in STREAMS:
        ready_unit(st)
    for st in STREAMS:
        both = pick_new(st)
        forward_start(1, st, both[:width], both[width:])
    send_out("f10")
    take_back("d0a")
    for st in STREAMS:
        backward_end(0, st, patch_out)
    for st in STREAMS:
        start_if(patches[2 + st])
    for st in STREAMS:
        ready_unit(2 + st)
    expert_forward("f10")
    for st in STREAMS:
        both = pick_new(2 + st)
        backward_start(1, st, both[:width], both[width:])
    send_out("d1b")
    forward_middle(1)
    for u in range(4):
        settle(u)
    expert_backward("d1b", "k1b")
    expert_forward("f11")
    backward_middle(1)
    take_back("f11")
    for st in STREAMS:
        forward_end(1, st, rows_out)
    expert_backward("d1a", "k1a")
    take_back("d1a")
    for st in STREAMS:
        backward_end(1, st, rows_out)

    for copy in pre_copies:
        copy.wait()
    for name in OUT:
        each_peer(lambda k, name=name: out_copy(name, k).wait_send())
    for name in BACK:
        each_peer(lambda k, name=name: back_copy(name, k).wait_send())
    for copy in pair_copies:
        copy.wait_send()
    for triple in bulk + patches + helds:
        @pl.when(triple[0])
        def _(triple=triple):
            triple[2].wait_send()


def merge(pre, rows, spread, out):
    out[0] = (pre[0].astype(F32) + mm(spread[0], rows[0])).astype(BF)


def local(sizes, state_in, entering, saved, route_ids, gate_vals, w_gate, w_up, w_down, gains):
    ns, ne, nd = sizes
    group, width = ne * nd // 2, ne // 2 * CAP
    units, tokens, model = state_in.shape[1:]
    hidden = w_gate.shape[-1]
    tables = route_ids.shape[1] * route_ids.shape[2] * route_ids.shape[3]
    topk = route_ids.shape[-1]
    turn = (0, 1, 2, 5, 3, 4)
    ids = jnp.transpose(route_ids, turn).reshape(tables * topk, tokens)
    gates = jnp.transpose(gate_vals, turn).reshape(tables * topk, tokens)
    vmem = pl.BlockSpec(memory_space=pltpu.VMEM)
    anywhere = pl.BlockSpec(memory_space=pl.ANY)
    dma = pltpu.SemaphoreType.DMA
    phases = len(OUT) + len(BACK)
    scratch = [
        pltpu.VMEM((len(OUT), ne, CAP, model), BF),
        pltpu.VMEM((len(OUT), group, CAP, model), BF),
        pltpu.VMEM((len(BACK), group, CAP, model), BF),
        pltpu.VMEM((len(BACK), group, CAP, model), BF),
        pltpu.VMEM((units, tokens, model), BF),
        pltpu.VMEM((units, tokens, model), BF),
        pltpu.VMEM((units, tokens, model), BF),
        pltpu.VMEM(saved.shape[1:], BF),
        pltpu.VMEM((units, 2 * width, model), BF),
        pltpu.VMEM((units, 2 * width, model), BF),
        pltpu.VMEM((units, 2 * width, tokens), BF),
        pltpu.VMEM((units, 2 * width, tokens), BF),
        pltpu.VMEM((tables, width, tokens), F32),
        pltpu.VMEM((tables, width, tokens), F32),
        pltpu.VMEM((12, width, 3 * width), F32),
        pltpu.VMEM((units, 2 * width, 2 * width), F32),
        pltpu.VMEM((units, 2 * width, model), F32),
        pltpu.VMEM((2 * len(VALS), width, model), F32),
        pltpu.VMEM((2 * len(INVS), width, tokens), F32),
        pltpu.VMEM((2 * len(PRES), group * CAP, 2 * hidden), F32),
        pltpu.VMEM((group * CAP, 2 * hidden), F32),
        pltpu.VMEM((2 * hidden, model), BF),
        pltpu.VMEM((2 * hidden, model), BF),
        pltpu.VMEM((2 * hidden, model), BF),
        dma((phases, group)), dma((phases, group)), dma((phases,)),
        dma((3, units)), dma((3, units)), dma((units,)), dma((3,)),
        dma((3,)), dma((3,)), dma((4,)), dma((units,)),
    ]
    pre, rows, spread = pl.pallas_call(
        functools.partial(kernel, sizes),
        out_shape=(
            jax.ShapeDtypeStruct((units, tokens, model), BF),
            jax.ShapeDtypeStruct((units, 2 * width, model), BF),
            jax.ShapeDtypeStruct((units, tokens, 2 * width), BF),
        ),
        in_specs=[anywhere, anywhere, anywhere, vmem, vmem, anywhere, anywhere, anywhere, vmem],
        out_specs=(anywhere, vmem, vmem),
        scratch_shapes=scratch,
        compiler_params=pltpu.CompilerParams(
            collective_id=0, has_side_effects=True, vmem_limit_bytes=67043328
        ),
    )(state_in[0], entering[0], saved[0], ids, gates, jnp.swapaxes(w_gate[0, 0], 0, 1),
      jnp.swapaxes(w_up[0, 0], 0, 1), w_down[0, 0], gains[0])
    result = pl.pallas_call(
        merge,
        grid=(units,),
        out_shape=jax.ShapeDtypeStruct((units, tokens, model), BF),
        in_specs=[
            pl.BlockSpec((1, tokens, model), lambda u: (u, 0, 0)),
            pl.BlockSpec((1, 2 * width, model), lambda u: (u, 0, 0)),
            pl.BlockSpec((1, tokens, 2 * width), lambda u: (u, 0, 0)),
        ],
        out_specs=pl.BlockSpec((1, tokens, model), lambda u: (u, 0, 0)),
    )(pre, rows, spread)
    return result[None]


def solution(mesh):
    in_specs = (
        P("segment", None, ("expert", "dp"), None),
        P(None, None, ("expert", "dp"), None),
        P("segment", None, None, ("expert", "dp"), None),
        P("segment", None, None, None, ("expert", "dp"), None),
        P("segment", None, None, None, ("expert", "dp"), None),
        P("segment", "expert", None, "dp"),
        P("segment", "expert", None, "dp"),
        P("segment", "expert", "dp", None),
        P("segment", None, None),
    )
    out_specs = P("segment", None, ("expert", "dp"), None)
    sizes = (mesh.shape["segment"], mesh.shape["expert"], mesh.shape["dp"])
    body = functools.partial(local, sizes)
    return jax.shard_map(body, mesh=mesh, in_specs=in_specs, out_specs=out_specs, check_vma=False)
```

time: 96.8 us -> 74.9 us (0.77)
  Pallas kernels: 86.3 us -> 74.6 us
  local copies, waits for them, and re-layouts: 10.2 us -> 0 us
    pallas_call x1 -> x2, Pallas kernels: 86.3 us -> 74.6 us  [the longest x1 70.3 us: local(): pl.pallas_call(functools.partial(kernel, sizes), out_shape=(jax.ShapeDtyp...]
    unnamed x7 -> x0, local copies, waits for them, and re-layouts: 10.2 us -> none
where the time goes in v1:
time: 74.9 us; the launch traced here: 74.6 us
  Pallas kernels  74.6 us (100%)
    pallas_call x1, Pallas kernels, local(): pl.pallas_call(functools.partial(kernel, sizes), out_shape=(jax.ShapeDtyp...  70.3 us
    pallas_call x1, Pallas kernels, local(): pl.pallas_call(merge, grid=(units,), out_shape=jax.ShapeDtypeStruct((unit...  4.33 us

profile of v1, /device:TPU:0, one launch (start us, length us, event | category | flops | bytes accessed | tf_op | source)
XLA Modules:
  0.0 74.6 jit_solution(2165929493576363785)
XLA Ops:
  0.0 70.3 %shard_map.91 = (bf16[4,128,2048]{2,1,0:T(8,128)(2,1)}, bf16[4,16,2048]{2,1,0:T(8,128)(2,1)}, bf16[4,128,16]{2,1,0:T(8,128)(2,1)}) custom-call(bf16[4,128,2048]{2,1,0:T(8,128)(2,1)} %bitcast.18, bf16[4,128,2048]{2,1,0:T(8,128)(2,1)} %bitcast.19, bf16[2,2,128,2048]{3,2,1,0:T(8,128)(2,1)} %bitcast.20, s32[96,128]{1,0:T(8,128)} %bitcast.24, ...), custom_call_target="tpu_custom_call" | custom-call | tf_op jit(solution)/shard_map/pallas_call | solution.py:603
  70.3 4.3 %shard_map.92 = bf16[4,128,2048]{2,1,0:T(8,128)(2,1)} custom-call(bf16[4,128,2048]{2,1,0:T(8,128)(2,1)} %get-tuple-element.8.pre, bf16[4,16,2048]{2,1,0:T(8,128)(2,1)} %get-tuple-element.9.rows, bf16[4,128,16]{2,1,0:T(8,128)(2,1)} %get-tuple-element.10.spread), custom_call_target="tpu_custom_call" | custom-call | tf_op jit(solution)/shard_map/pallas_call | solution.py:618

commit v2 on v1

--- a/solution.py
+++ b/solution.py
@@ -28,6 +28,10 @@
     return lax.dot_general(a, b, LAST, preferred_element_type=F32)
 
 
+def mm_flip(rows, weights):
+    return lax.dot_general(weights, rows, LAST, preferred_element_type=F32).T
+
+
 def mix(picks, rows):
     high = rows.astype(BF).astype(F32)
     rest = rows - high
@@ -55,12 +59,12 @@
     return a % b if isinstance(a, int) else lax.rem(a, b)
 
 
-def kernel(sizes, state_in, entering, saved_in, ids, gates, wg_in, wu_in, wd_in, gains,
-           pre_out, rows_out, spread_out,
-           outs, ins, bouts, bins, base, final, state, saved, patch_out, patch_in, held_out, held_in,
+def kernel(sizes, state_in, entering, saved_in, ids_in, gates_in, wg_in, wu_in, wd_in, gains_in,
+           final, rows_out, spread_out,
+           outs, ins, bouts, bins, base, ids, gates, gains, state, saved, patch_out, patch_in, held_out, held_in,
            sel, gate_col, overlaps, moves, fresh_base, vals, invs, pre, early, wg, wu, wd,
-           send_sem, recv_sem, local_sem, relay_send, relay_recv, enter_sem, weight_sem,
-           pair_send, pair_recv, input_sem, pre_sem):
+           send_sem, recv_sem, relay_send, relay_recv, enter_sem, weight_sem,
+           pair_send, pair_recv, input_sem, small_sem):
     ns, ne, nd = sizes
     nh = nd // 2
     group = ne * nh
@@ -68,6 +72,8 @@
     width = ec * CAP
     tokens, model = state_in.shape[1], state_in.shape[2]
     hidden = wg_in.shape[0]
+    hm = model // 2
+    gr = group * CAP
     seg, ex, dp = lax.axis_index("segment"), lax.axis_index("expert"), lax.axis_index("dp")
     half, side = lax.div(dp, 2), lax.rem(dp, 2)
     me = ex * nh + half
@@ -77,7 +83,11 @@
         pltpu.make_async_copy(state_in.at[pl.ds(2 * i, 2)], state.at[pl.ds(2 * i, 2)], input_sem.at[2 + i])
         for i in range(2)
     ]
-    for copy in (saved_copies[0], state_copies[0], state_copies[1]):
+    small_copies = [
+        pltpu.make_async_copy(source, dest, small_sem.at[i])
+        for i, (source, dest) in enumerate(((ids_in, ids), (gates_in, gates), (gains_in, gains)))
+    ]
+    for copy in (*small_copies, saved_copies[0]):
         copy.start()
 
     barrier = pltpu.get_barrier_semaphore()
@@ -92,12 +102,7 @@
     def peer(k):
         te = lax.rem(ex + quotient(k, nh), ne)
         th = lax.rem(half + remainder(k, nh), nh)
-        return te, th, (seg, te, th * 2 + side)
-
-    def source_of(k):
-        te = lax.rem(ex - quotient(k, nh) + ne, ne)
-        th = lax.rem(half - remainder(k, nh) + nh, nh)
-        return te * nh + th
+        return te, th, (seg, te, th * 2 + 1 - side)
 
     partner = (seg, ex, half * 2 + 1 - side)
     has_up, has_down = seg < ns - 1, seg > 0
@@ -128,9 +133,8 @@
         )
         for i, (source, dest) in enumerate(weights)
     ]
-    for copy in weight_copies:
+    for copy in (state_copies[0], *weight_copies, saved_copies[1], state_copies[1]):
         copy.start()
-    saved_copies[1].start()
 
     units = state_in.shape[0]
     lane = lax.broadcasted_iota(jnp.int32, (tokens, tokens), 1)
@@ -144,6 +148,8 @@
     def tab(slot, unit, sub):
         return sub * su + slot * units + unit
 
+    small_copies[0].wait()
+    small_copies[1].wait()
     for e in range(ec):
         routed, weight = [], []
         for j in range(2):
@@ -166,11 +172,6 @@
                 jnp.sum(one * weight[tb:tb + 1], axis=1, keepdims=True), (CAP, tokens)
             )
 
-    neighbours = jnp.where(has_up, 1, 0) + jnp.where(has_down, 1, 0)
-    pl.semaphore_wait(barrier, group + neighbours)
-    for copy in pair_copies:
-        copy.start()
-
     def first_second(slot, unit):
         first = unit % 2
         return sel[tab(slot, unit, first)], sel[tab(slot, unit, 1 - first)]
@@ -202,7 +203,7 @@
         goes, comes = (has_up, has_down) if up else (has_down, has_up)
         target = lax.rem(seg + (1 if up else ns - 1), ns)
         copy = pltpu.make_async_remote_copy(
-            src_ref=source, dst_ref=dest, send_sem=relay_send.at[kind, unit],
+            src_ref=source, dst_ref=dest, send_sem=relay_send.at[kind, 0 if up else 1],
             recv_sem=relay_recv.at[kind, unit], device_id=(target, ex, dp), device_id_type=MESH,
         )
         return goes, comes, copy
@@ -219,8 +220,8 @@
 
     bulk = [relay(u, 0, state_in.at[u], base.at[u]) for u in range(4)]
     enter = [pltpu.make_async_copy(entering.at[u], base.at[u], enter_sem.at[u]) for u in range(4)]
-    patches = [relay(u, 1, patch_out.at[u], patch_in.at[u]) for u in range(4)]
-    helds = [relay(u, 2, held_out.at[u], held_in.at[u]) for u in range(4)]
+    patches = [[relay(u, 1 + i, patch_out.at[u, i], patch_in.at[u, i]) for i in range(2)] for u in range(4)]
+    helds = [relay(u, 3, held_out.at[u], held_in.at[u]) for u in range(4)]
 
     def wait_bulk(u):
         arrive_if(bulk[u])
@@ -229,62 +230,50 @@
         def _():
             enter[u].wait()
 
-    def out_copy(name, k):
+    def out_copy(name, hf, k):
         i = OUT.index(name)
         te, th, device = peer(k)
         return pltpu.make_async_remote_copy(
-            src_ref=outs.at[i, te], dst_ref=ins.at[i, me], send_sem=send_sem.at[i, k],
-            recv_sem=recv_sem.at[i, k], device_id=device, device_id_type=MESH,
+            src_ref=outs.at[i, hf, te], dst_ref=ins.at[i, hf, me], send_sem=send_sem.at[i],
+            recv_sem=recv_sem.at[i, hf], device_id=device, device_id_type=MESH,
         )
 
-    def back_copy(name, k):
+    def back_copy(name, hf, k):
         i = BACK.index(name)
         te, th, device = peer(k)
         return pltpu.make_async_remote_copy(
-            src_ref=bouts.at[i, te * nh + th], dst_ref=bins.at[i, me], send_sem=send_sem.at[len(OUT) + i, k],
-            recv_sem=recv_sem.at[len(OUT) + i, k], device_id=device, device_id_type=MESH,
+            src_ref=bouts.at[i, hf, te * nh + th], dst_ref=bins.at[i, hf, me], send_sem=send_sem.at[len(OUT) + i],
+            recv_sem=recv_sem.at[len(OUT) + i, hf], device_id=device, device_id_type=MESH,
         )
 
-    def own_out(name):
+    def send_out(name):
         i = OUT.index(name)
-        return pltpu.make_async_copy(outs.at[i, ex], ins.at[i, me], local_sem.at[i])
-
-    def own_back(name):
+        for hf in range(2):
+            each_peer(lambda k, hf=hf: out_copy(name, hf, k).start())
+        for hf in range(2):
+            pltpu.make_async_copy(outs.at[i, hf, ex], ins.at[i, hf, me], recv_sem.at[i, hf]).start()
+
+    def send_back(name, hf):
         i = BACK.index(name)
-        return pltpu.make_async_copy(bouts.at[i, me], bins.at[i, me], local_sem.at[len(OUT) + i])
-
-    def send_out(name):
-        each_peer(lambda k: out_copy(name, k).start())
-        own_out(name).start()
-
-    def send_back(name):
-        each_peer(lambda k: back_copy(name, k).start())
-        own_back(name).start()
-
-    def arrived(buffer, i, phase):
-        def body(k):
-            slot = buffer.at[i, source_of(k)]
-            pltpu.make_async_remote_copy(
-                src_ref=slot, dst_ref=slot, send_sem=send_sem.at[phase, k],
-                recv_sem=recv_sem.at[phase, k], device_id=peer(k)[2], device_id_type=MESH,
-            ).wait_recv()
-
-        each_peer(body)
-
-    def take_out(name):
+        each_peer(lambda k: back_copy(name, hf, k).start())
+        pltpu.make_async_copy(bouts.at[i, hf, me], bins.at[i, hf, me], recv_sem.at[len(OUT) + i, hf]).start()
+
+    def take_out(name, hf):
         i = OUT.index(name)
-        own_out(name).wait()
-        arrived(ins, i, i)
+        pltpu.make_async_copy(ins.at[i, hf], ins.at[i, hf], recv_sem.at[i, hf]).wait()
 
     def take_back(name):
         i = BACK.index(name)
-        own_back(name).wait()
-        arrived(bins, i, len(OUT) + i)
+        for hf in range(2):
+            pltpu.make_async_copy(bins.at[i, hf], bins.at[i, hf], recv_sem.at[len(OUT) + i, hf]).wait()
 
     def put(name, unit, second, rows):
         j = 1 - unit % 2 if second else unit % 2
         for e in range(ec):
-            outs[OUT.index(name), j * ec + e] = rows[e * CAP:(e + 1) * CAP].astype(BF)
+            for hf in range(2):
+                outs[OUT.index(name), hf, j * ec + e] = (
+                    rows[e * CAP:(e + 1) * CAP, hf * hm:(hf + 1) * hm].astype(BF)
+                )
 
     def got(name, unit, second):
         j = 1 - unit % 2 if second else unit % 2
@@ -292,29 +281,62 @@
         parts = []
         for e in range(ec):
             first = (j * ec + e) * nh
-            total = bins[i, first].astype(F32)
-            for q in range(1, nh):
-                total = total + bins[i, first + q].astype(F32)
-            parts.append(total)
+            halves = []
+            for hf in range(2):
+                total = bins[i, hf, first].astype(F32)
+                for q in range(1, nh):
+                    total = total + bins[i, hf, first + q].astype(F32)
+                halves.append(total)
+            parts.append(jnp.concatenate(halves, axis=1))
         return parts[0] if ec == 1 else jnp.concatenate(parts)
 
-    def rows_of(name):
-        return ins[OUT.index(name)].astype(F32).reshape(group * CAP, model).astype(BF)
-
-    def give(name, rows):
-        bouts[BACK.index(name)] = rows.reshape(group, CAP, model).astype(BF)
-
-    def half_forward(rows):
-        return mm_t(rows, wg[...]), mm_t(rows, wu[...])
-
-    def finish_forward(gp, up):
-        return mm((gp * jax.nn.sigmoid(gp) * up).astype(BF), wd[...])
-
-    def backward(act, gp, up):
+    def rows_of(hf, *names):
+        parts = [ins[OUT.index(name), hf].astype(F32).reshape(gr, hm) for name in names]
+        return (parts[0] if len(parts) == 1 else jnp.concatenate(parts)).astype(BF)
+
+    def give(name, hf, rows):
+        bouts[BACK.index(name), hf] = rows.reshape(group, CAP, hm).astype(BF)
+
+    def cut(weight, hf):
+        return weight[:, hf * hm:(hf + 1) * hm]
+
+    def inward(weights, *names, ready=None):
+        product = mm_t if len(names) == 1 else mm_flip
+        sums = [None] * len(weights)
+        if ready is None:
+            for hf in range(2):
+                for name in names:
+                    take_out(name, hf)
+                rows = rows_of(hf, *names)
+                for i, weight in enumerate(weights):
+                    part = product(rows, cut(weight, hf))
+                    sums[i] = part if hf == 0 else sums[i] + part
+            return sums
+        for hf in range(2):
+            for name in names:
+                take_out(name, hf)
+        for i, weight in enumerate(weights):
+            ready(i)
+            sums[i] = product(rows_of(0, *names), cut(weight, 0)) + product(rows_of(1, *names), cut(weight, 1))
+        return sums
+
+    def activate(gp, up):
+        return (gp * jax.nn.sigmoid(gp) * up).astype(BF)
+
+    def outward(names, pairs):
+        for hf in range(2):
+            total = mm(pairs[0][0], cut(pairs[0][1], hf))
+            for a, weight in pairs[1:]:
+                total = total + mm(a, cut(weight, hf))
+            for n, name in enumerate(names):
+                give(name, hf, total[n * gr:(n + 1) * gr])
+                send_back(name, hf)
+
+    def backward(name, act, gp, up):
         sig = jax.nn.sigmoid(gp)
         grad_gate = (act * up * sig * (1.0 + gp * (1.0 - sig))).astype(BF)
         grad_up = (act * gp * sig).astype(BF)
-        return mm(grad_gate, wg[...]) + mm(grad_up, wu[...])
+        outward((name,), ((grad_gate, wg), (grad_up, wu)))
 
     def at(name, st):
         return VALS.index(name) * 2 + st
@@ -355,7 +377,6 @@
             rows, inv = unit_norm(both[:width], gain(b, False))
             put(name, b, False, rows)
             keep_inv(slot, "a", st, inv)
-        send_out(name)
 
     def middle_kept(slot):
         take_back(f"k{slot}a")
@@ -373,6 +394,10 @@
         vals[at("fx1", st)], vals[at("fx2", st)] = first, second
         put(f"f{slot}0", st, False, unit_norm(first, gain(st, False))[0])
 
+    def send_patch(u, part, rows):
+        patch_out[u, part] = rows.astype(BF)
+        start_if(patches[u][part])
+
     def forward_middle(slot):
         take_back(f"f{slot}0")
         for st in STREAMS:
@@ -383,9 +408,8 @@
             put(f"f{slot}1", st, True, unit_norm(middle, gain(st, True))[0])
         send_out(f"f{slot}1")
 
-    def forward_end(slot, st, dest):
-        second = vals[at("fx2", st)] + gate(slot, st, True) * got(f"f{slot}1", st, True)
-        dest[st] = jnp.concatenate([vals[at("fx1", st)], second]).astype(BF)
+    def forward_end(slot, st):
+        return vals[at("fx2", st)] + gate(slot, st, True) * got(f"f{slot}1", st, True)
 
     def backward_start(slot, st, first, second):
         vals[at(f"d{slot}a", st)], vals[at(f"d{slot}b", st)] = first, second
@@ -404,57 +428,70 @@
             vals[at(f"d{slot}a", st)] = inner
         send_out(f"d{slot}a")
 
-    def backward_end(slot, st, dest):
+    def backward_end(slot, st):
         b = 2 + st
-        first = vals[at(f"d{slot}a", st)] + back_norm(
+        return vals[at(f"d{slot}a", st)] + back_norm(
             vals[at(f"k{slot}a", st)], held_inv(slot, "a", st), gain(b, False), got(f"d{slot}a", b, False)
         )
-        dest[b] = jnp.concatenate([first, vals[at(f"d{slot}b", st)]]).astype(BF)
-
-    def expert_forward(name, kept=False):
-        take_out(name)
-        gp, up = half_forward(rows_of(name))
-        if kept:
-            keep_pre(name, (gp, up))
-        give(name, finish_forward(gp, up))
-        send_back(name)
+
+    def expert_forward(name):
+        gp, up = inward((wg, wu), name)
+        outward((name,), ((activate(gp, up), wd),))
 
     def expert_backward(name, pres):
-        take_out(name)
-        give(name, backward(mm_t(rows_of(name), wd[...]), *pre_at(pres)))
-        send_back(name)
+        act, = inward((wd,), name)
+        backward(name, act, *pre_at(pres))
 
     def ready_unit(u):
+        last = 1 if u < 2 else 0
         wait_bulk(u)
         arrive_if(helds[u])
+        arrive_if(patches[u][1 - last])
         held = held_in[u].astype(F32)
         both = both_picks(1, u)
         keep = 1.0 - jnp.sum(held, axis=0, keepdims=True)
-        moves[u] = mm_t(both.astype(BF), held.astype(BF))
-        fresh_base[u] = mm((both * keep).astype(BF), base[u])
+        parts = [mm_t(both.astype(BF), held[i * width:(i + 1) * width].astype(BF)) for i in range(2)]
+        moves[u] = parts[last]
+        fresh_base[u] = mm((both * keep).astype(BF), base[u]) + mm(parts[1 - last].astype(BF), patch_in[u, 1 - last])
 
     def pick_new(u):
-        arrive_if(patches[u])
-        return fresh_base[u] + mm(moves[u].astype(BF), patch_in[u])
-
-    pre_copies = [pltpu.make_async_copy(final.at[u], pre_out.at[u], pre_sem.at[u]) for u in range(4)]
-
-    def settle(u):
+        last = 1 if u < 2 else 0
+        arrive_if(patches[u][last])
+        return fresh_base[u] + mm(moves[u].astype(BF), patch_in[u, last])
+
+    def settle(u, parts):
         new_sel = last_picks(1, u)
         fresh = 1.0 - jnp.sum(new_sel, axis=0, keepdims=True)
         old_sel = held_in[u].astype(F32) * fresh
         kept = eye * (fresh - jnp.sum(old_sel, axis=0, keepdims=True))
-        spread = mm_t(eye.astype(BF), jnp.concatenate([old_sel, new_sel]).astype(BF))
-        spread_out[u] = spread[:, 2 * width:].astype(BF)
-        final[u] = (mm(kept.astype(BF), base[u]) + mm(spread[:, :2 * width].astype(BF), patch_in[u])).astype(BF)
-        pre_copies[u].start()
-
+        picks = [old_sel] + [new_sel[i * width:(i + 1) * width] for i, _ in parts]
+        rows = [patch_in[u, i].astype(F32) for i in range(2)] + [value for _, value in parts]
+        spread = mm_t(eye.astype(BF), jnp.concatenate(picks).astype(BF))
+        final[u] = (
+            mm(kept.astype(BF), base[u]) + mm(spread.astype(BF), jnp.concatenate(rows).astype(BF))
+        ).astype(BF)
+        if u >= 2:
+            spread_out[u - 2] = mm_t(eye.astype(BF), new_sel[:width].astype(BF)).astype(BF)
+
+    def drain(*phases):
+        for phase in phases:
+            sent = ins.at[0, :, pl.ds(0, group - 1)]
+            pltpu.make_async_copy(sent, sent, send_sem.at[phase]).wait()
+
+    neighbours = jnp.where(has_up, 1, 0) + jnp.where(has_down, 1, 0)
+    pl.semaphore_wait(barrier, group + neighbours)
+    for copy in pair_copies:
+        copy.start()
+    small_copies[2].wait()
     start_kept(0)
+    send_out("k0a")
     state_copies[0].wait()
     for st in STREAMS:
         both = pick(0, st, state[st])
         forward_start(0, st, both[:width], both[width:])
     send_out("f00")
+    start_kept(1)
+    send_out("k1a")
     state_copies[1].wait()
     for st in STREAMS:
         both = pick(0, 2 + st, state[2 + st])
@@ -482,30 +519,34 @@
             if u >= 2:
                 overlaps[over_at(slot, u, True)] = crossing(slot, u, True)
 
-    for i in range(3):
+    def wait_weight(i):
         weight_copies[i].wait()
         pair_copies[i].wait_recv()
-    expert_forward("k0a", True)
-    expert_forward("f00")
-    start_kept(1)
-    take_out("d0b")
-    early[...] = mm_t(rows_of("d0b"), wd[...])
+
+    gp, up = inward((wg, wu), "k0a", ready=wait_weight)
+    keep_pre("k0a", (gp, up))
+    wait_weight(2)
+    outward(("k0a",), ((activate(gp, up), wd),))
+    gp, up = inward((wg, wu), "f00", "k1a")
+    outward(("f00", "k1a"), ((activate(gp, up), wd),))
+    keep_pre("k1a", (gp[gr:], up[gr:]))
     middle_kept(0)
     forward_middle(0)
-    expert_forward("k1a", True)
-    take_out("k0b")
-    give("d0b", backward(early[...], *half_forward(rows_of("k0b"))))
-    send_back("d0b")
-    expert_forward("f01")
+    for st in STREAMS:
+        send_patch(st, 0, vals[at("fx1", st)])
+    early[...], = inward((wd,), "d0b")
     middle_kept(1)
+    gp, up = inward((wg, wu), "k0b")
+    backward("d0b", early[...], gp, up)
+    gp, up = inward((wg, wu), "f01", "k1b")
+    outward(("f01",), ((activate(gp[:gr], up[:gr]), wd),))
+    keep_pre("k1b", (gp[gr:], up[gr:]))
     backward_middle(0)
+    for st in STREAMS:
+        send_patch(2 + st, 1, vals[at("d0b", st)])
     take_back("f01")
     for st in STREAMS:
-        forward_end(0, st, patch_out)
-    for st in STREAMS:
-        start_if(patches[st])
-    take_out("k1b")
-    keep_pre("k1b", half_forward(rows_of("k1b")))
+        send_patch(st, 1, forward_end(0, st))
     expert_backward("d0a", "k0a")
     for st in STREAMS:
         ready_unit(st)
@@ -513,48 +554,56 @@
         both = pick_new(st)
         forward_start(1, st, both[:width], both[width:])
     send_out("f10")
+    for st in STREAMS:
+        ready_unit(2 + st)
     take_back("d0a")
     for st in STREAMS:
-        backward_end(0, st, patch_out)
-    for st in STREAMS:
-        start_if(patches[2 + st])
-    for st in STREAMS:
-        ready_unit(2 + st)
+        send_patch(2 + st, 0, backward_end(0, st))
     expert_forward("f10")
     for st in STREAMS:
         both = pick_new(2 + st)
         backward_start(1, st, both[:width], both[width:])
     send_out("d1b")
     forward_middle(1)
-    for u in range(4):
-        settle(u)
     expert_backward("d1b", "k1b")
     expert_forward("f11")
     backward_middle(1)
+    for st in STREAMS:
+        settle(2 + st, [(1, vals[at("d1b", st)])])
     take_back("f11")
     for st in STREAMS:
-        forward_end(1, st, rows_out)
+        settle(st, [(0, vals[at("fx1", st)]), (1, forward_end(1, st))])
     expert_backward("d1a", "k1a")
-    take_back("d1a")
-    for st in STREAMS:
-        backward_end(1, st, rows_out)
-
-    for copy in pre_copies:
-        copy.wait()
-    for name in OUT:
-        each_peer(lambda k, name=name: out_copy(name, k).wait_send())
-    for name in BACK:
-        each_peer(lambda k, name=name: back_copy(name, k).wait_send())
+    last = len(OUT) + len(BACK) - 1
+    drain(*range(last))
     for copy in pair_copies:
         copy.wait_send()
-    for triple in bulk + patches + helds:
-        @pl.when(triple[0])
-        def _(triple=triple):
-            triple[2].wait_send()
-
-
-def merge(pre, rows, spread, out):
-    out[0] = (pre[0].astype(F32) + mm(spread[0], rows[0])).astype(BF)
+    for goes, way in ((has_up, 0), (has_down, 1)):
+        @pl.when(goes)
+        def _(way=way):
+            pairs = (base.at[pl.ds(0, 2)], patch_in.at[0], patch_in.at[0], held_in.at[pl.ds(0, 2)])
+            for kind, sent in enumerate(pairs):
+                pltpu.make_async_copy(sent, sent, relay_send.at[kind, way]).wait()
+    take_back("d1a")
+    for st in STREAMS:
+        rows_out[st] = backward_end(1, st).astype(BF)
+    drain(last)
+
+
+def merge(final, rows, spread, out, merged, out_sem):
+    units = final.shape[0]
+    sources = [final.at[u] if u < 2 else merged.at[u - 2] for u in range(units)]
+    copies = [pltpu.make_async_copy(sources[u], out.at[u], out_sem.at[u]) for u in range(units)]
+    for u in range(units):
+        if u >= 2:
+            merged[u - 2] = (final[u].astype(F32) + mm(spread[u - 2], rows[u - 2])).astype(BF)
+        copies[u].start()
+    for copy in copies:
+        copy.wait()
+
+
+def stay(value):
+    return pltpu.with_memory_space_constraint(value, pltpu.HBM)
 
 
 def local(sizes, state_in, entering, saved, route_ids, gate_vals, w_gate, w_up, w_down, gains):
@@ -572,22 +621,24 @@
     dma = pltpu.SemaphoreType.DMA
     phases = len(OUT) + len(BACK)
     scratch = [
-        pltpu.VMEM((len(OUT), ne, CAP, model), BF),
-        pltpu.VMEM((len(OUT), group, CAP, model), BF),
-        pltpu.VMEM((len(BACK), group, CAP, model), BF),
-        pltpu.VMEM((len(BACK), group, CAP, model), BF),
+        pltpu.VMEM((len(OUT), 2, ne, CAP, model // 2), BF),
+        pltpu.VMEM((len(OUT), 2, group, CAP, model // 2), BF),
+        pltpu.VMEM((len(BACK), 2, group, CAP, model // 2), BF),
+        pltpu.VMEM((len(BACK), 2, group, CAP, model // 2), BF),
         pltpu.VMEM((units, tokens, model), BF),
-        pltpu.VMEM((units, tokens, model), BF),
+        pltpu.VMEM(ids.shape, jnp.int32),
+        pltpu.VMEM(gates.shape, F32),
+        pltpu.VMEM(gains.shape[1:], F32),
         pltpu.VMEM((units, tokens, model), BF),
         pltpu.VMEM(saved.shape[1:], BF),
-        pltpu.VMEM((units, 2 * width, model), BF),
-        pltpu.VMEM((units, 2 * width, model), BF),
+        pltpu.VMEM((units, 2, width, model), BF),
+        pltpu.VMEM((units, 2, width, model), BF),
         pltpu.VMEM((units, 2 * width, tokens), BF),
         pltpu.VMEM((units, 2 * width, tokens), BF),
         pltpu.VMEM((tables, width, tokens), F32),
         pltpu.VMEM((tables, width, tokens), F32),
         pltpu.VMEM((12, width, 3 * width), F32),
-        pltpu.VMEM((units, 2 * width, 2 * width), F32),
+        pltpu.VMEM((units, 2 * width, width), F32),
         pltpu.VMEM((units, 2 * width, model), F32),
         pltpu.VMEM((2 * len(VALS), width, model), F32),
         pltpu.VMEM((2 * len(INVS), width, tokens), F32),
@@ -596,36 +647,37 @@
         pltpu.VMEM((2 * hidden, model), BF),
         pltpu.VMEM((2 * hidden, model), BF),
         pltpu.VMEM((2 * hidden, model), BF),
-        dma((phases, group)), dma((phases, group)), dma((phases,)),
-        dma((3, units)), dma((3, units)), dma((units,)), dma((3,)),
-        dma((3,)), dma((3,)), dma((4,)), dma((units,)),
+        dma((phases,)), dma((phases, 2)),
+        dma((4, 2)), dma((4, units)), dma((units,)), dma((3,)),
+        dma((3,)), dma((3,)), dma((4,)), dma((3,)),
     ]
-    pre, rows, spread = pl.pallas_call(
+    final, rows, spread = pl.pallas_call(
         functools.partial(kernel, sizes),
         out_shape=(
             jax.ShapeDtypeStruct((units, tokens, model), BF),
-            jax.ShapeDtypeStruct((units, 2 * width, model), BF),
-            jax.ShapeDtypeStruct((units, tokens, 2 * width), BF),
+            jax.ShapeDtypeStruct((2, width, model), BF),
+            jax.ShapeDtypeStruct((2, tokens, width), BF),
         ),
-        in_specs=[anywhere, anywhere, anywhere, vmem, vmem, anywhere, anywhere, anywhere, vmem],
-        out_specs=(anywhere, vmem, vmem),
+        in_specs=[anywhere] * 9,
+        out_specs=(vmem, vmem, vmem),
         scratch_shapes=scratch,
         compiler_params=pltpu.CompilerParams(
-            collective_id=0, has_side_effects=True, vmem_limit_bytes=67043328
+            collective_id=0, has_side_effects=True, vmem_limit_bytes=(44 if ne <= 4 else 60) * 1024 * 1024
         ),
-    )(state_in[0], entering[0], saved[0], ids, gates, jnp.swapaxes(w_gate[0, 0], 0, 1),
-      jnp.swapaxes(w_up[0, 0], 0, 1), w_down[0, 0], gains[0])
+    )(*map(stay, (
+        state_in[0], entering[0], saved[0], ids, gates, jnp.swapaxes(w_gate[0, 0], 0, 1),
+        jnp.swapaxes(w_up[0, 0], 0, 1), w_down[0, 0], gains[0],
+    )))
     result = pl.pallas_call(
         merge,
-        grid=(units,),
         out_shape=jax.ShapeDtypeStruct((units, tokens, model), BF),
-        in_specs=[
-            pl.BlockSpec((1, tokens, model), lambda u: (u, 0, 0)),
-            pl.BlockSpec((1, 2 * width, model), lambda u: (u, 0, 0)),
-            pl.BlockSpec((1, tokens, 2 * width), lambda u: (u, 0, 0)),
+        in_specs=[vmem] * 3,
+        out_specs=pl.BlockSpec(memory_space=pltpu.HBM),
+        scratch_shapes=[
+            pltpu.VMEM((units - 2, tokens, model), BF), dma((units,)),
         ],
-        out_specs=pl.BlockSpec((1, tokens, model), lambda u: (u, 0, 0)),
-    )(pre, rows, spread)
+        compiler_params=pltpu.CompilerParams(vmem_limit_bytes=8 * 1024 * 1024),
+    )(final, rows, spread)
     return result[None]
 
 

time: 74.9 us -> 64.5 us (0.86)
  Pallas kernels: 74.6 us -> 64.2 us
    pallas_call x1, Pallas kernels: 70.3 us -> 62.8 us  [local(): pl.pallas_call(functools.partial(kernel, sizes), out_shape=(jax.ShapeDtyp...]
    pallas_call x1, Pallas kernels: 4.33 us -> 1.35 us  [local(): pl.pallas_call(merge, out_shape=jax.ShapeDtypeStruct((units, tokens, mode...]
where the time goes in v2:
time: 64.5 us; the launch traced here: 64.4 us
  Pallas kernels  64.2 us (100%)
    pallas_call x1, Pallas kernels, local(): pl.pallas_call(functools.partial(kernel, sizes), out_shape=(jax.ShapeDtyp...  62.8 us
    pallas_call x1, Pallas kernels, local(): pl.pallas_call(merge, out_shape=jax.ShapeDtypeStruct((units, tokens, mode...  1.35 us

profile of v2, /device:TPU:0, one launch (start us, length us, event | category | flops | bytes accessed | tf_op | source)
XLA Modules:
  0.0 64.4 jit_solution(8916693487479315944)
XLA Ops:
  0.0 62.8 %shard_map.91 = (bf16[4,128,2048]{2,1,0:T(8,128)(2,1)S(1)}, bf16[2,8,2048]{2,1,0:T(8,128)(2,1)S(1)}, bf16[2,128,8]{2,1,0:T(8,128)(2,1)S(1)}) custom-call(bf16[4,128,2048]{2,1,0:T(8,128)(2,1)} %bitcast.18, bf16[4,128,2048]{2,1,0:T(8,128)(2,1)} %bitcast.19, bf16[2,2,128,2048]{3,2,1,0:T(8,128)(2,1)} %bitcast.20, s32[96,128]{1,0:T(8,128)} %bitcast.24, ...), custom_call_target="tpu_custom_call" | custom-call | tf_op jit(solution)/shard_map/pallas_call | solution.py:654
  62.8 1.3 %shard_map.92 = bf16[4,128,2048]{2,1,0:T(8,128)(2,1)} custom-call(bf16[4,128,2048]{2,1,0:T(8,128)(2,1)S(1)} %get-tuple-element.8.final, bf16[2,8,2048]{2,1,0:T(8,128)(2,1)S(1)} %get-tuple-element.9.rows, bf16[2,128,8]{2,1,0:T(8,128)(2,1)S(1)} %get-tuple-element.10.spread), custom_call_target="tpu_custom_call" | custom-call | tf_op jit(solution)/shard_map/pallas_call | solution.py:671

commit v3 on v2

--- a/solution.py
+++ b/solution.py
@@ -28,10 +28,6 @@
     return lax.dot_general(a, b, LAST, preferred_element_type=F32)
 
 
-def mm_flip(rows, weights):
-    return lax.dot_general(weights, rows, LAST, preferred_element_type=F32).T
-
-
 def mix(picks, rows):
     high = rows.astype(BF).astype(F32)
     rest = rows - high
@@ -62,8 +58,8 @@
 def kernel(sizes, state_in, entering, saved_in, ids_in, gates_in, wg_in, wu_in, wd_in, gains_in,
            final, rows_out, spread_out,
            outs, ins, bouts, bins, base, ids, gates, gains, state, saved, patch_out, patch_in, held_out, held_in,
-           sel, gate_col, overlaps, moves, fresh_base, vals, invs, pre, early, wg, wu, wd,
-           send_sem, recv_sem, relay_send, relay_recv, enter_sem, weight_sem,
+           sel, gate_col, overlaps, moves, fresh_base, vals, invs, pre, early, hold, wg, wu, wd, wgn, wun, wdn,
+           send_sem, recv_sem, back_sem, relay_send, relay_recv, weight_sem,
            pair_send, pair_recv, input_sem, small_sem):
     ns, ne, nd = sizes
     nh = nd // 2
@@ -126,12 +122,15 @@
         pltpu.make_async_copy(source, dest.at[pl.ds(0, hidden)], weight_sem.at[i])
         for i, (source, dest) in enumerate(weights)
     ]
+    pieces = [(source, dest.at[pl.ds(hidden, hidden)]) for source, dest in weights[:2]] + [
+        (wd_in.at[:, pl.ds(hf * hm, hm)], wd.at[pl.ds(hidden, hidden), pl.ds(hf * hm, hm)]) for hf in range(2)
+    ]
     pair_copies = [
         pltpu.make_async_remote_copy(
-            src_ref=source, dst_ref=dest.at[pl.ds(hidden, hidden)], send_sem=pair_send.at[i],
+            src_ref=source, dst_ref=dest, send_sem=pair_send.at[i],
             recv_sem=pair_recv.at[i], device_id=partner, device_id_type=MESH,
         )
-        for i, (source, dest) in enumerate(weights)
+        for i, (source, dest) in enumerate(pieces)
     ]
     for copy in (state_copies[0], *weight_copies, saved_copies[1], state_copies[1]):
         copy.start()
@@ -219,7 +218,7 @@
             triple[2].wait_recv()
 
     bulk = [relay(u, 0, state_in.at[u], base.at[u]) for u in range(4)]
-    enter = [pltpu.make_async_copy(entering.at[u], base.at[u], enter_sem.at[u]) for u in range(4)]
+    enter = [pltpu.make_async_copy(entering.at[u], base.at[u], relay_recv.at[0, u]) for u in range(4)]
     patches = [[relay(u, 1 + i, patch_out.at[u, i], patch_in.at[u, i]) for i in range(2)] for u in range(4)]
     helds = [relay(u, 3, held_out.at[u], held_in.at[u]) for u in range(4)]
 
@@ -234,7 +233,7 @@
         i = OUT.index(name)
         te, th, device = peer(k)
         return pltpu.make_async_remote_copy(
-            src_ref=outs.at[i, hf, te], dst_ref=ins.at[i, hf, me], send_sem=send_sem.at[i],
+            src_ref=outs.at[i, hf, te], dst_ref=ins.at[i, hf, me], send_sem=send_sem.at[0],
             recv_sem=recv_sem.at[i, hf], device_id=device, device_id_type=MESH,
         )
 
@@ -242,8 +241,8 @@
         i = BACK.index(name)
         te, th, device = peer(k)
         return pltpu.make_async_remote_copy(
-            src_ref=bouts.at[i, hf, te * nh + th], dst_ref=bins.at[i, hf, me], send_sem=send_sem.at[len(OUT) + i],
-            recv_sem=recv_sem.at[len(OUT) + i, hf], device_id=device, device_id_type=MESH,
+            src_ref=bouts.at[i, hf, te * nh + th], dst_ref=bins.at[i, hf, me], send_sem=send_sem.at[1 if i + 1 < len(BACK) else 2],
+            recv_sem=back_sem.at[i], device_id=device, device_id_type=MESH,
         )
 
     def send_out(name):
@@ -256,7 +255,7 @@
     def send_back(name, hf):
         i = BACK.index(name)
         each_peer(lambda k: back_copy(name, hf, k).start())
-        pltpu.make_async_copy(bouts.at[i, hf, me], bins.at[i, hf, me], recv_sem.at[len(OUT) + i, hf]).start()
+        pltpu.make_async_copy(bouts.at[i, hf, me], bins.at[i, hf, me], back_sem.at[i]).start()
 
     def take_out(name, hf):
         i = OUT.index(name)
@@ -264,8 +263,7 @@
 
     def take_back(name):
         i = BACK.index(name)
-        for hf in range(2):
-            pltpu.make_async_copy(bins.at[i, hf], bins.at[i, hf], recv_sem.at[len(OUT) + i, hf]).wait()
+        pltpu.make_async_copy(bins.at[i], bins.at[i], back_sem.at[i]).wait()
 
     def put(name, unit, second, rows):
         j = 1 - unit % 2 if second else unit % 2
@@ -300,31 +298,42 @@
     def cut(weight, hf):
         return weight[:, hf * hm:(hf + 1) * hm]
 
+    def turn(source, dest):
+        for c in range(0, model, 256):
+            dest[c:c + 256] = source[:, c:c + 256].T
+
+    def product(rows, weight, hf):
+        if weight.shape[0] == model:
+            return mm(rows, weight[hf * hm:(hf + 1) * hm])
+        return mm_t(rows, cut(weight, hf))
+
     def inward(weights, *names, ready=None):
-        product = mm_t if len(names) == 1 else mm_flip
         sums = [None] * len(weights)
-        if ready is None:
-            for hf in range(2):
-                for name in names:
-                    take_out(name, hf)
-                rows = rows_of(hf, *names)
-                for i, weight in enumerate(weights):
-                    part = product(rows, cut(weight, hf))
-                    sums[i] = part if hf == 0 else sums[i] + part
-            return sums
         for hf in range(2):
             for name in names:
                 take_out(name, hf)
-        for i, weight in enumerate(weights):
-            ready(i)
-            sums[i] = product(rows_of(0, *names), cut(weight, 0)) + product(rows_of(1, *names), cut(weight, 1))
+            if ready is not None:
+                continue
+            rows = rows_of(hf, *names)
+            for i, weight in enumerate(weights):
+                part = product(rows, weight, hf)
+                if hf == 0:
+                    hold[i, :len(names) * gr] = part
+                else:
+                    sums[i] = part + hold[i, :len(names) * gr]
+        if ready is not None:
+            for i, weight in enumerate(weights):
+                ready(i)
+                sums[i] = product(rows_of(0, *names), weight, 0) + product(rows_of(1, *names), weight, 1)
         return sums
 
     def activate(gp, up):
         return (gp * jax.nn.sigmoid(gp) * up).astype(BF)
 
-    def outward(names, pairs):
+    def outward(names, pairs, ready=None):
         for hf in range(2):
+            if ready is not None:
+                ready(2 + hf)
             total = mm(pairs[0][0], cut(pairs[0][1], hf))
             for a, weight in pairs[1:]:
                 total = total + mm(a, cut(weight, hf))
@@ -434,12 +443,12 @@
             vals[at(f"k{slot}a", st)], held_inv(slot, "a", st), gain(b, False), got(f"d{slot}a", b, False)
         )
 
-    def expert_forward(name):
-        gp, up = inward((wg, wu), name)
+    def expert_forward(name, weights):
+        gp, up = inward(weights, name)
         outward((name,), ((activate(gp, up), wd),))
 
     def expert_backward(name, pres):
-        act, = inward((wd,), name)
+        act, = inward((wdn,), name)
         backward(name, act, *pre_at(pres))
 
     def ready_unit(u):
@@ -473,10 +482,9 @@
         if u >= 2:
             spread_out[u - 2] = mm_t(eye.astype(BF), new_sel[:width].astype(BF)).astype(BF)
 
-    def drain(*phases):
-        for phase in phases:
-            sent = ins.at[0, :, pl.ds(0, group - 1)]
-            pltpu.make_async_copy(sent, sent, send_sem.at[phase]).wait()
+    def drain(buffer, i):
+        sent = buffer.at[:, :, pl.ds(0, group - 1)]
+        pltpu.make_async_copy(sent, sent, send_sem.at[i]).wait()
 
     neighbours = jnp.where(has_up, 1, 0) + jnp.where(has_down, 1, 0)
     pl.semaphore_wait(barrier, group + neighbours)
@@ -520,34 +528,40 @@
                 overlaps[over_at(slot, u, True)] = crossing(slot, u, True)
 
     def wait_weight(i):
-        weight_copies[i].wait()
+        if i < 3:
+            weight_copies[i].wait()
         pair_copies[i].wait_recv()
 
     gp, up = inward((wg, wu), "k0a", ready=wait_weight)
     keep_pre("k0a", (gp, up))
-    wait_weight(2)
-    outward(("k0a",), ((activate(gp, up), wd),))
-    gp, up = inward((wg, wu), "f00", "k1a")
-    outward(("f00", "k1a"), ((activate(gp, up), wd),))
+    outward(("k0a",), ((activate(gp, up), wd),), wait_weight)
+    expert_forward("f00", (wg, wu))
+    middle_kept(0)
+    turn(wd, wdn)
+    early[...], = inward((wdn,), "d0b")
+    turn(wg, wgn)
+    turn(wu, wun)
+    gp, up = inward((wgn, wun), "k0b")
+    backward("d0b", early[...], gp, up)
+    forward_middle(0)
+    for st in STREAMS:
+        send_patch(st, 0, vals[at("fx1", st)])
+    backward_middle(0)
+    for st in STREAMS:
+        send_patch(2 + st, 1, vals[at("d0b", st)])
+    gp, up = inward((wgn, wun), "f01", "k1a")
+    outward(("f01", "k1a"), ((activate(gp, up), wd),))
     keep_pre("k1a", (gp[gr:], up[gr:]))
-    middle_kept(0)
-    forward_middle(0)
-    for st in STREAMS:
-        send_patch(st, 0, vals[at("fx1", st)])
-    early[...], = inward((wd,), "d0b")
+    expert_backward("d0a", "k0a")
+    take_back("f01")
+    for st in STREAMS:
+        send_patch(st, 1, forward_end(0, st))
+    for st in STREAMS:
+        ready_unit(2 + st)
     middle_kept(1)
-    gp, up = inward((wg, wu), "k0b")
-    backward("d0b", early[...], gp, up)
-    gp, up = inward((wg, wu), "f01", "k1b")
-    outward(("f01",), ((activate(gp[:gr], up[:gr]), wd),))
-    keep_pre("k1b", (gp[gr:], up[gr:]))
-    backward_middle(0)
-    for st in STREAMS:
-        send_patch(2 + st, 1, vals[at("d0b", st)])
-    take_back("f01")
-    for st in STREAMS:
-        send_patch(st, 1, forward_end(0, st))
-    expert_backward("d0a", "k0a")
+    take_back("d0a")
+    for st in STREAMS:
+        send_patch(2 + st, 0, backward_end(0, st))
     for st in STREAMS:
         ready_unit(st)
     for st in STREAMS:
@@ -555,27 +569,24 @@
         forward_start(1, st, both[:width], both[width:])
     send_out("f10")
     for st in STREAMS:
-        ready_unit(2 + st)
-    take_back("d0a")
-    for st in STREAMS:
-        send_patch(2 + st, 0, backward_end(0, st))
-    expert_forward("f10")
-    for st in STREAMS:
         both = pick_new(2 + st)
         backward_start(1, st, both[:width], both[width:])
     send_out("d1b")
+    gp, up = inward((wgn, wun), "f10", "k1b")
+    outward(("f10",), ((activate(gp[:gr], up[:gr]), wd),))
+    keep_pre("k1b", (gp[gr:], up[gr:]))
+    expert_backward("d1b", "k1b")
     forward_middle(1)
-    expert_backward("d1b", "k1b")
-    expert_forward("f11")
     backward_middle(1)
+    expert_forward("f11", (wgn, wun))
+    expert_backward("d1a", "k1a")
     for st in STREAMS:
         settle(2 + st, [(1, vals[at("d1b", st)])])
     take_back("f11")
     for st in STREAMS:
         settle(st, [(0, vals[at("fx1", st)]), (1, forward_end(1, st))])
-    expert_backward("d1a", "k1a")
-    last = len(OUT) + len(BACK) - 1
-    drain(*range(last))
+    drain(ins, 0)
+    drain(bins.at[pl.ds(0, len(BACK) - 1)], 1)
     for copy in pair_copies:
         copy.wait_send()
     for goes, way in ((has_up, 0), (has_down, 1)):
@@ -587,7 +598,7 @@
     take_back("d1a")
     for st in STREAMS:
         rows_out[st] = backward_end(1, st).astype(BF)
-    drain(last)
+    drain(bins.at[pl.ds(0, 1)], 2)
 
 
 def merge(final, rows, spread, out, merged, out_sem):
@@ -619,7 +630,6 @@
     vmem = pl.BlockSpec(memory_space=pltpu.VMEM)
     anywhere = pl.BlockSpec(memory_space=pl.ANY)
     dma = pltpu.SemaphoreType.DMA
-    phases = len(OUT) + len(BACK)
     scratch = [
         pltpu.VMEM((len(OUT), 2, ne, CAP, model // 2), BF),
         pltpu.VMEM((len(OUT), 2, group, CAP, model // 2), BF),
@@ -644,12 +654,16 @@
         pltpu.VMEM((2 * len(INVS), width, tokens), F32),
         pltpu.VMEM((2 * len(PRES), group * CAP, 2 * hidden), F32),
         pltpu.VMEM((group * CAP, 2 * hidden), F32),
+        pltpu.VMEM((2, 2 * group * CAP, 2 * hidden), F32),
         pltpu.VMEM((2 * hidden, model), BF),
         pltpu.VMEM((2 * hidden, model), BF),
         pltpu.VMEM((2 * hidden, model), BF),
-        dma((phases,)), dma((phases, 2)),
-        dma((4, 2)), dma((4, units)), dma((units,)), dma((3,)),
-        dma((3,)), dma((3,)), dma((4,)), dma((3,)),
+        pltpu.VMEM((model, 2 * hidden), BF),
+        pltpu.VMEM((model, 2 * hidden), BF),
+        pltpu.VMEM((model, 2 * hidden), BF),
+        dma((3,)), dma((len(OUT), 2)), dma((len(BACK),)),
+        dma((4, 2)), dma((4, units)), dma((3,)),
+        dma((4,)), dma((4,)), dma((4,)), dma((3,)),
     ]
     final, rows, spread = pl.pallas_call(
         functools.partial(kernel, sizes),
@@ -662,7 +676,7 @@
         out_specs=(vmem, vmem, vmem),
         scratch_shapes=scratch,
         compiler_params=pltpu.CompilerParams(
-            collective_id=0, has_side_effects=True, vmem_limit_bytes=(44 if ne <= 4 else 60) * 1024 * 1024
+            collective_id=0, has_side_effects=True, vmem_limit_bytes=46137344 if ne <= 4 else 67043328
         ),
     )(*map(stay, (
         state_in[0], entering[0], saved[0], ids, gates, jnp.swapaxes(w_gate[0, 0], 0, 1),

time: 64.5 us -> 55.2 us (0.86)
  Pallas kernels: 64.2 us -> 54.8 us
    pallas_call x1, Pallas kernels: 62.8 us -> 53.5 us  [local(): pl.pallas_call(functools.partial(kernel, sizes), out_shape=(jax.ShapeDtyp...]
where the time goes in v3:
time: 55.2 us; the launch traced here: 55 us
  Pallas kernels  54.8 us (99%)
    pallas_call x1, Pallas kernels, local(): pl.pallas_call(functools.partial(kernel, sizes), out_shape=(jax.ShapeDtyp...  53.5 us
    pallas_call x1, Pallas kernels, local(): pl.pallas_call(merge, out_shape=jax.ShapeDtypeStruct((units, tokens, mode...  1.35 us

profile of v3, /device:TPU:0, one launch (start us, length us, event | category | flops | bytes accessed | tf_op | source)
XLA Modules:
  0.0 55.0 jit_solution(8763048020570347022)
XLA Ops:
  0.0 53.5 %shard_map.91 = (bf16[4,128,2048]{2,1,0:T(8,128)(2,1)S(1)}, bf16[2,8,2048]{2,1,0:T(8,128)(2,1)S(1)}, bf16[2,128,8]{2,1,0:T(8,128)(2,1)S(1)}) custom-call(bf16[4,128,2048]{2,1,0:T(8,128)(2,1)} %bitcast.18, bf16[4,128,2048]{2,1,0:T(8,128)(2,1)} %bitcast.19, bf16[2,2,128,2048]{3,2,1,0:T(8,128)(2,1)} %bitcast.20, s32[96,128]{1,0:T(8,128)} %bitcast.24, ...), custom_call_target="tpu_custom_call" | custom-call | tf_op jit(solution)/shard_map/pallas_call | solution.py:668
  53.5 1.3 %shard_map.92 = bf16[4,128,2048]{2,1,0:T(8,128)(2,1)} custom-call(bf16[4,128,2048]{2,1,0:T(8,128)(2,1)S(1)} %get-tuple-element.8.final, bf16[2,8,2048]{2,1,0:T(8,128)(2,1)S(1)} %get-tuple-element.9.rows, bf16[2,128,8]{2,1,0:T(8,128)(2,1)S(1)} %get-tuple-element.10.spread), custom_call_target="tpu_custom_call" | custom-call | tf_op jit(solution)/shard_map/pallas_call | solution.py:685
